TPU v7x, 32 devices: a whole 2x2x4 slice. The times are simulated.
32 devices in a mesh: tm: 8 (over z, y), pair: 4 (over x, core).
Axes of the slice: x: 2, y: 2, z: 4, core: 2. Of those that a mesh axis runs over, the one named last changes fastest.
Arguments:
- x_series: float32 [128, 32768], P('pair', 'tm'), may hold values from -6 to 6
- y_series: float32 [128, 32768], P('pair', 'tm'), may hold values from -6 to 6
Outputs:
- correlation: float32 [128, 512], P('tm', 'pair')
All inputs are finite; a program needn't handle non-finite values.
Results may differ from a plain program's by a relative error of at most 0.000082.
Values sent between devices are 32-bit elements; how exact they have to be, the bound alone decides.
No kernel may reach another device: no remote copies, remote signals or barrier semaphores. Data moves between devices by JAX's collectives and lax.ppermute only.
A program may use at most 64 MiB of HBM per device.

v0:
```python
import math

import jax
import jax.numpy as jnp
from jax import lax
from jax.sharding import PartitionSpec as P

L = 512


def passed_along(array, axis, by):
    devices = lax.axis_size(axis)
    pairs = [(i, i + by) for i in range(devices) if 0 <= i + by < devices]
    return lax.ppermute(array, axis, pairs)


def lag_products(series, extended):
    block_len = min(128, L)
    pair_count, length = series.shape
    block_rows = length // block_len
    left_rows = series.reshape(pair_count, block_rows, block_len)
    pieces = [
        extended[:, offset * block_len : offset * block_len + length].reshape(
            pair_count, block_rows, block_len
        )
        for offset in range(L // block_len + 1)
    ]
    right_rows = jnp.concatenate(pieces, axis=2)
    grams = jnp.einsum(
        "pbi,pbj->pij",
        left_rows,
        right_rows,
        precision=lax.Precision.HIGHEST,
        preferred_element_type=jnp.float32,
    )
    span_cols = L + block_len
    flattened = grams.reshape(pair_count, block_len * span_cols)
    flattened = jnp.pad(flattened, ((0, 0), (0, block_len)))
    skewed = flattened.reshape(pair_count, block_len, span_cols + 1)
    return jnp.sum(skewed[:, :, :L], axis=1)


def per_block(members):
    return lag_products(members[0], members[1])


def body(x_series, y_series):
    head_rows = y_series[:, :L]
    incoming = passed_along(head_rows, "tm", -1)
    extended = jnp.concatenate([y_series, incoming], axis=1)
    pairs_here, length = x_series.shape
    group_size = min(32, pairs_here)
    block_count = pairs_here // group_size
    partial_value = lax.map(
        per_block,
        (
            x_series.reshape(block_count, group_size, length),
            extended.reshape(block_count, group_size, length + L),
        ),
    )
    partial_value = partial_value.reshape(pairs_here, L)
    norm_scale = 1.0 / math.sqrt(lax.axis_size("tm") * length)
    regrouped = lax.all_to_all(partial_value, "pair", split_axis=1, concat_axis=0, tiled=True)
    lagged = lax.psum_scatter(regrouped, "tm", scatter_dimension=0, tiled=True)
    return lagged * norm_scale


def solution(mesh):
    in_specs = (P("pair", "tm"), P("pair", "tm"))
    out_specs = P("tm", "pair")
    return jax.shard_map(body, mesh=mesh, in_specs=in_specs, out_specs=out_specs, check_vma=False)
```

profile of v0, /device:TPU:0, one launch (start us, length us, event | category | flops | bytes accessed | tf_op | source)
XLA Modules:
  0.0 153.1 jit_solution(17430132601227821452)
XLA Ops:
  6.5 0.0 reduce-scatter.2.cloned.1.call-start
  6.5 0.8 slice.25
  7.4 1.3 collective-permute-start
  8.7 1.1 constant_dynamic-update-slice_fusion.1
  9.8 1.1 copy.14
  10.9 1.1 copy.9
  12.1 2.4 %collective-permute-done = f32[32,512]{1,0:T(8,128)S(1)} collective-permute-done((f32[32,512]{1,0:T(8,128)S(1)}, f32[32,512]{1,0:T(8,128)S(1)}, u32[]{:S(2)}, u32[]{:S(2)}) %collective-permute-start) | collective-permute-done | bytes 65568 | tf_op jit(solution)/shard_map/ppermute | solution.py:14
  14.5 0.1 slice_bitcast_fusion
  14.7 0.1 copy.13
  14.8 0.1 copy.12
  14.9 0.1 copy.11
  15.0 0.1 copy.10
  15.2 19.0 %convolution_bitcast_fusion = f32[32,128,640]{1,2,0:T(8,128)} fusion(f32[32,32,640]{2,1,0:T(8,128)S(1)} %constant_dynamic-update-slice_fusion.2, f32[32,32,128]{2,1,0:T(8,128)S(1)} %bitcast.39), kind=kOutput, calls=%fused_computation.1 | convolution fusion | flops 1006632960 | bytes 13631488 | tf_op jit(solution)/shard_map/while/body/eval_jaxpr/pbi,pbj->pij/dot_general | solution.py:29
  34.3 12.2 %copy.15 = f32[4,8,128,640]{3,1,2,0:T(8,128)} copy(f32[4,8,128,640]{2,3,1,0:T(8,128)} %bitcast.31) | data formatting | bytes 20971520
  46.5 8.6 %pad.5 = f32[32,82048]{1,0:T(8,128)} pad(f32[32,81920]{1,0:T(8,128)} %bitcast.32, f32[]{:T(128)} %constant.8.clone.1), padding=0_0x0_128 | pad | bytes 20987908 | tf_op jit(solution)/shard_map/while/body/eval_jaxpr/jit(_pad)/pad | solution.py:38
  55.0 14.9 %reshape.51 = f32[32,128,641]{2,1,0:T(8,128)} reshape(f32[32,82048]{1,0:T(8,128)} %pad.5) | data formatting | bytes 21004288 | tf_op jit(solution)/shard_map/while/body/eval_jaxpr/reshape | solution.py:39
  69.9 4.5 %slice_reduce_fusion = f32[32,512]{1,0:T(8,128)S(1)} fusion(f32[32,128,641]{2,1,0:T(8,128)} %reshape.51), kind=kLoop, calls=%fused_computation | loop fusion | flops 2080768 | bytes 8454144 | tf_op jit(solution)/shard_map/while/body/eval_jaxpr/reduce_sum | solution.py:40
  74.5 7.3 %all_to_all.19 = f32[32,4,128]{2,0,1:T(8,128)} all-to-all(f32[32,4,128]{2,0,1:T(8,128)S(1)} %copy_bitcast_fusion), channel_id=1, replica_groups=mesh['tm'=8,'pair'=4] {'pair'}, dimensions={1} | all-to-all | bytes 131072 | tf_op jit(solution)/shard_map/all_to_all | solution.py:63
  81.8 0.0 reduce-scatter.2.cloned.1.call-update
  81.8 63.2 %reduce-scatter.2.cloned.1.call-done = f32[16,128]{1,0:T(8,128)} async-done(((f32[128,128]{1,0:T(8,128)}), f32[16,128]{1,0:T(8,128)}) %reduce-scatter.2.cloned.1.call-update) | async-done | bytes 8208 | tf_op jit(solution)/shard_map/reduce_scatter | solution.py:64
  145.0 1.3 broadcast_multiply_fusion
  (7 shorter events, 0.2 us)
Async XLA Ops:
  6.5 138.5 %reduce-scatter.2.cloned.1.call-start = ((), (), s32[]{:S(2)}) async-start(), calls=%async_computation.2 | async-start | bytes 73728 | tf_op jit(solution)/shard_map/reduce_scatter | solution.py:64
  7.4 7.1 %collective-permute-start = (f32[32,512]{1,0:T(8,128)S(1)}, f32[32,512]{1,0:T(8,128)S(1)}, u32[]{:S(2)}, u32[]{:S(2)}) collective-permute-start(f32[32,512]{1,0:T(8,128)S(1)} %slice.25), channel_id=1, source_target_pairs={{4,0},{8,4},{12,8},{16,12},{20,16},{24,20},{28,24},{5,1},{9,5},{13... | collective-permute-start | bytes 196616 | tf_op jit(solution)/shard_map/ppermute | solution.py:14
Sparse Core Ops, SparseCore 0:
  81.9 63.0 reduce-scatter.1
where the time goes:
time: 154 us; the launch traced here: 153 us
  waiting for transfers between devices  65.6 us (43%)
  local copies, waits for them, and re-layouts  40.6 us (26%)
  matrix products  19 us (12%)
  between operations  13.5 us (9%)
  blocking collectives  7.28 us (5%)
  other arithmetic  5.83 us (4%)
    reduce_scatter x1, waiting for transfers between devices, body(): lagged = lax.psum_scatter(regrouped, 'tm', scatter_dimension=0, tiled=True)  63.2 us
    dot_general x1, matrix products, lag_products(): jnp.einsum('pbi,pbj->pij', left_rows, right_rows, precision=lax.Precision...  19 us
    unnamed x13, local copies, waits for them, and re-layouts  16.2 us
    reshape x1, local copies, waits for them, and re-layouts, lag_products(): skewed = flattened.reshape(pair_count, block_len, span_cols + 1)  14.9 us
    pad x1, local copies, waits for them, and re-layouts, lag_products(): flattened = jnp.pad(flattened, ((0, 0), (0, block_len)))  8.56 us
    all_to_all x1, blocking collectives, body(): lax.all_to_all(partial_value, 'pair', split_axis=1, concat_axis=0, tiled=...  7.28 us
    reduce_sum x1, other arithmetic, lag_products(): return jnp.sum(skewed[:, :, :L], axis=1)  4.53 us
  transfers between devices with their start and end apart: 2, of which 2 were waited for; matrix products, arithmetic and copies ran while one was open for 2% of the time, Pallas kernels for 0%

commit v1 on v0

v1 whole, which is shorter than its diff:
```python
import functools
import math

import jax
import jax.numpy as jnp
from jax import lax
from jax.experimental import pallas as pl
from jax.experimental.pallas import tpu as pltpu
from jax.sharding import PartitionSpec as P

L = 512
LANES = 128
SUB = 8


def gram_kernel(x_ref, y_ref, h_ref, o_ref, hi_ref, lo_ref):
    rows = y_ref.shape[1]
    blocks = rows // SUB
    shifts = L // LANES + 1
    width = shifts * LANES
    for ref, at in ((y_ref, 0), (h_ref, rows)):
        value = ref[0]
        high = value.astype(jnp.bfloat16).astype(jnp.float32)
        hi_ref[at : at + value.shape[0], :] = high
        lo_ref[at : at + value.shape[0], :] = value - high
    sub_index = lax.broadcasted_iota(jnp.int32, (SUB, width), 0)
    for p in range(SUB):
        x = x_ref[0, pl.ds(p, blocks, stride=SUB), :]
        x_high = x.astype(jnp.bfloat16).astype(jnp.float32)
        left = jnp.concatenate([x_high, x_high, x - x_high], axis=0)
        left = left.T.astype(jnp.bfloat16)
        highs, lows = [], []
        for o in range(shifts):
            at = pl.ds(p + SUB * o, blocks, stride=SUB)
            highs.append(hi_ref[at, :].astype(jnp.bfloat16))
            lows.append(lo_ref[at, :].astype(jnp.bfloat16))
        highs = jnp.concatenate(highs, axis=1)
        lows = jnp.concatenate(lows, axis=1)
        right = jnp.concatenate([highs, lows, highs], axis=0)
        grams = jnp.dot(left, right, preferred_element_type=jnp.float32)
        total = grams[0:SUB]
        for a in range(1, LANES // SUB):
            piece = grams[a * SUB : (a + 1) * SUB]
            total = total + pltpu.roll(piece, width - a * SUB, 1)
        for bit in (4, 2, 1):
            moved = pltpu.roll(total, width - bit, 1)
            total = jnp.where((sub_index & bit) != 0, moved, total)
        o_ref[p : p + 1, :] = jnp.sum(total[:, :L], axis=0, keepdims=True)


def tiles_of(array):
    pairs_here, length = array.shape
    groups, blocks = pairs_here // SUB, length // LANES
    tiles = array.reshape(groups, SUB, blocks, LANES).transpose(0, 2, 1, 3)
    return tiles.reshape(groups, blocks * SUB, LANES)


def lag_products(x, y, halo):
    pairs_here, length = x.shape
    groups, blocks = pairs_here // SUB, length // LANES
    halo_blocks = L // LANES
    whole = pl.BlockSpec((1, blocks * SUB, LANES), lambda g: (g, 0, 0))
    edge = pl.BlockSpec((1, halo_blocks * SUB, LANES), lambda g: (g, 0, 0))
    scratch = pltpu.VMEM(((blocks + halo_blocks) * SUB, LANES), jnp.float32)
    return pl.pallas_call(
        gram_kernel,
        grid=(groups,),
        in_specs=[whole, whole, edge],
        out_specs=pl.BlockSpec((SUB, L), lambda g: (g, 0)),
        out_shape=jax.ShapeDtypeStruct((pairs_here, L), jnp.float32),
        scratch_shapes=[scratch, scratch],
    )(tiles_of(x), tiles_of(y), tiles_of(halo))


def body(x, y):
    tm, pair = lax.axis_size("tm"), lax.axis_size("pair")
    halo = lax.ppermute(y[:, :L], "tm", [(i, i - 1) for i in range(1, tm)])
    partial = lag_products(x, y, halo)
    pairs_here, length = x.shape
    out_rows = pairs_here * pair // tm
    out_cols = L // pair
    blocks_here = pairs_here // out_rows
    mine = partial.reshape(blocks_here, out_rows, pair, out_cols).transpose(0, 2, 1, 3)
    send = jnp.zeros((tm, pair, out_rows, out_cols), jnp.float32)
    place = lax.axis_index("pair") * blocks_here
    send = lax.dynamic_update_slice(send, mine, (place, 0, 0, 0))
    send = send.reshape(tm * pair, out_rows, out_cols)
    received = lax.all_to_all(send, ("tm", "pair"), 0, 0, tiled=True)
    return jnp.sum(received, axis=0) * (1.0 / math.sqrt(tm * length))


def solution(mesh):
    specs = (P("pair", "tm"), P("pair", "tm"))
    return jax.shard_map(
        body, mesh=mesh, in_specs=specs, out_specs=P("tm", "pair"), check_vma=False
    )
```

time: 154 us -> 36.8 us (0.24)
  waiting for transfers between devices: 65.6 us -> 5.84 us
  local copies, waits for them, and re-layouts: 40.6 us -> 2.36 us
  matrix products: 19 us -> 0 us
  between operations: 13.5 us -> 0.04 us
  Pallas kernels: 0 us -> 9.8 us
  blocking collectives: 7.28 us -> 16.6 us
  other arithmetic: 5.83 us -> 0.64 us
    reduce_scatter x1 -> x0, waiting for transfers between devices: 63.2 us -> none  [body(): lagged = lax.psum_scatter(regrouped, 'tm', scatter_dimension=0, tiled=True)]
    dot_general x1 -> x0, matrix products: 19 us -> none  [lag_products(): jnp.einsum('pbi,pbj->pij', left_rows, right_rows, precision=lax.Precision...]
    unnamed x13 -> x2, local copies, waits for them, and re-layouts: 16.2 us -> 0.62 us
    reshape x1, local copies, waits for them, and re-layouts: 14.9 us -> 0.86 us  [body(): partial.reshape(blocks_here, out_rows, pair, out_cols).transpose(0, 2, 1, 3)]
    pallas_call x0 -> x1, Pallas kernels: none -> 9.8 us  [lag_products(): pl.pallas_call(gram_kernel, grid=(groups,), in_specs=[whole, whole, edge]...]
    all_to_all x1, blocking collectives: 7.28 us -> 16.6 us  [body(): received = lax.all_to_all(send, ('tm', 'pair'), 0, 0, tiled=True)]
    pad x1 -> x0, local copies, waits for them, and re-layouts: 8.56 us -> none  [lag_products(): flattened = jnp.pad(flattened, ((0, 0), (0, block_len)))]
    reduce_sum x1, other arithmetic: 4.53 us -> 0.04 us  [body(): return jnp.sum(received, axis=0) * (1.0 / math.sqrt(tm * length))]
  transfers between devices with their start and end apart: 2 -> 1, of which waited for: 2 -> 1; matrix products, arithmetic and copies ran while one was open for 2% -> 0% of each run, Pallas kernels for 0% -> 0%
where the time goes in v1:
time: 36.8 us; the launch traced here: 36.6 us
  blocking collectives  16.6 us (45%)
  Pallas kernels  9.8 us (27%)
  waiting for transfers between devices  5.84 us (16%)
  local copies, waits for them, and re-layouts  2.36 us (6%)
  starting transfers between devices  1.28 us (3%)
  other arithmetic  0.64 us (2%)
    all_to_all x1, blocking collectives, body(): received = lax.all_to_all(send, ('tm', 'pair'), 0, 0, tiled=True)  16.6 us
    pallas_call x1, Pallas kernels, lag_products(): pl.pallas_call(gram_kernel, grid=(groups,), in_specs=[whole, whole, edge]...  9.8 us
    ppermute x1, waiting for transfers between devices, body(): halo = lax.ppermute(y[:, :L], 'tm', [(i, i - 1) for i in range(1, tm)])  5.84 us
    ppermute x1, starting transfers between devices, body(): halo = lax.ppermute(y[:, :L], 'tm', [(i, i - 1) for i in range(1, tm)])  1.28 us
    reshape x1, local copies, waits for them, and re-layouts, body(): partial.reshape(blocks_here, out_rows, pair, out_cols).transpose(0, 2, 1, 3)  0.86 us
    slice x1, local copies, waits for them, and re-layouts, body(): halo = lax.ppermute(y[:, :L], 'tm', [(i, i - 1) for i in range(1, tm)])  0.84 us
  transfers between devices with their start and end apart: 1, of which 1 were waited for; matrix products, arithmetic and copies ran while one was open for 0% of the time, Pallas kernels for 0%

profile of v1, /device:TPU:0, one launch (start us, length us, event | category | flops | bytes accessed | tf_op | source)
XLA Modules:
  0.0 36.6 jit_solution(14155050979347752816)
XLA Ops:
  0.0 0.8 %slice.3 = f32[32,512]{1,0:T(8,128)S(1)} slice(f32[32,4096]{1,0:T(8,128)} %param.3), slice={[0:32], [0:512]} | slice | bytes 131072 | tf_op jit(solution)/shard_map/slice | solution.py:77
  0.8 1.3 %collective-permute-start = (f32[32,512]{1,0:T(8,128)S(1)}, f32[32,512]{1,0:T(8,128)S(1)}, u32[]{:S(2)}, u32[]{:S(2)}) collective-permute-start(f32[32,512]{1,0:T(8,128)S(1)} %slice.3), channel_id=1, source_target_pairs={{4,0},{8,4},{12,8},{16,12},{20,16},{24,20},{28,24},{5,1},{9,5},{13... | collective-permute-start | bytes 196616 | tf_op jit(solution)/shard_map/ppermute | solution.py:77
  2.1 5.8 %collective-permute-done = f32[32,512]{1,0:T(8,128)S(1)} collective-permute-done((f32[32,512]{1,0:T(8,128)S(1)}, f32[32,512]{1,0:T(8,128)S(1)}, u32[]{:S(2)}, u32[]{:S(2)}) %collective-permute-start) | collective-permute-done | bytes 65568 | tf_op jit(solution)/shard_map/ppermute | solution.py:77
  8.0 0.0 copy-start
  8.0 0.6 %copy-done = f32[32,512]{1,0:T(8,128)} copy-done((f32[32,512]{1,0:T(8,128)}, f32[32,512]{1,0:T(8,128)S(1)}, u32[]{:S(2)}) %copy-start) | copy-done | bytes 65560
  8.6 9.8 %shard_map.28 = f32[32,512]{1,0:T(8,128)} custom-call(f32[4,256,128]{2,1,0:T(8,128)} %bitcast.20, f32[4,256,128]{2,1,0:T(8,128)} %bitcast.19, f32[4,32,128]{2,1,0:T(8,128)} %bitcast.21), custom_call_target="tpu_custom_call" | custom-call | tf_op jit(solution)/shard_map/pallas_call | solution.py:65
  18.4 0.9 %reshape.30 = f32[2,16,4,128]{3,2,1,0:T(4,128)S(1)} reshape(f32[32,512]{1,0:T(8,128)} %shard_map.28) | data formatting | bytes 131072 | tf_op jit(solution)/shard_map/reshape | solution.py:83
  19.3 16.6 %all_to_all.5 = f32[32,16,128]{2,1,0:T(8,128)S(1)} all-to-all(f32[32,16,128]{2,1,0:T(8,128)S(1)} %bitcast.18), channel_id=1, replica_groups=mesh['tm'=8,'pair'=4] {'tm','pair'}, dimensions={0} | all-to-all | bytes 524288 | tf_op jit(solution)/shard_map/all_to_all | solution.py:88
  36.0 0.6 %broadcast_multiply_fusion = f32[16,128]{1,0:T(8,128)} fusion(f32[16,128]{1,0:T(8,128)S(1)} %reduce_sum.9), kind=kLoop, calls=%fused_computation.1 | loop fusion | flops 2048 | bytes 16384 | tf_op jit(solution)/shard_map/mul | solution.py:89
  (3 shorter events, 0.1 us)
Async XLA Ops:
  0.8 7.1 %collective-permute-start = (f32[32,512]{1,0:T(8,128)S(1)}, f32[32,512]{1,0:T(8,128)S(1)}, u32[]{:S(2)}, u32[]{:S(2)}) collective-permute-start(f32[32,512]{1,0:T(8,128)S(1)} %slice.3), channel_id=1, source_target_pairs={{4,0},{8,4},{12,8},{16,12},{20,16},{24,20},{28,24},{5,1},{9,5},{13... | collective-permute-start | bytes 196616 | tf_op jit(solution)/shard_map/ppermute | solution.py:77
  8.0 0.6 %copy-start = (f32[32,512]{1,0:T(8,128)}, f32[32,512]{1,0:T(8,128)S(1)}, u32[]{:S(2)}) copy-start(f32[32,512]{1,0:T(8,128)S(1)} %collective-permute-done) | copy-start | bytes 196612

commit v2 on v1

v2 whole, which is shorter than its diff:
```python
import math

import jax
import jax.numpy as jnp
from jax import lax
from jax.experimental import pallas as pl
from jax.experimental.pallas import tpu as pltpu
from jax.sharding import PartitionSpec as P

L = 512
LANES = 128
SUB = 8
HALF = LANES // 2
FINE = 16


def split(value):
    high = value.astype(jnp.bfloat16)
    return high, (value - high.astype(jnp.float32)).astype(jnp.bfloat16)


def split_wide(value):
    high = value.astype(jnp.bfloat16).astype(jnp.float32)
    return high, value - high


def lane_index(shape):
    return lax.broadcasted_iota(jnp.int32, shape, 1)


def store_tiles(ref, p, value):
    for o in range(ref.shape[0]):
        ref[o, p * SUB : (p + 1) * SUB, :] = value[:, o * LANES : (o + 1) * LANES]


def strided_tiles(ref, s):
    at = pl.ds(s, SUB, stride=SUB)
    return jnp.concatenate([ref[o, at, :] for o in range(ref.shape[0])], axis=1)


def load_kernel(x_hbm, y_hbm, x_ref, y_ref, head_ref, sems):
    fetch_y = pltpu.make_async_copy(y_hbm, y_ref, sems.at[0])
    fetch_x = pltpu.make_async_copy(x_hbm, x_ref, sems.at[1])
    fetch_y.start()
    fetch_x.start()
    fetch_y.wait()
    head_ref[...] = y_ref[:, : head_ref.shape[1], :]
    fetch_x.wait()


def main_kernel(scale, x_ref, y_ref, o_ref, th_ref, tl_ref, *scratch):
    def step(g, carry):
        main_group(g, scale, x_ref, y_ref, o_ref, th_ref, tl_ref, *scratch)
        return carry

    lax.fori_loop(0, x_ref.shape[0], step, 0)


def main_group(g, scale, x_ref, y_ref, o_ref, th_ref, tl_ref, xr_ref, eh, el, oh, ol, tot):
    rows = y_ref.shape[1]
    blocks = rows // SUB
    shifts = L // LANES + 1
    width = shifts * LANES
    edge = (shifts - 1) * SUB
    x = x_ref[g]
    xr_ref[...] = pltpu.roll(x, HALF, 1)
    y = y_ref[g]
    y_rolled = pltpu.roll(y, HALF, 1)
    nothing = jnp.zeros((SUB, LANES), jnp.float32)
    y_next = jnp.concatenate([y_rolled[SUB:], nothing], axis=0)
    y_odd = jnp.where(lane_index(y.shape) < HALF, y_rolled, y_next)
    for value, high_ref, low_ref in ((y, eh, el), (y_odd, oh, ol)):
        high, low = split_wide(value)
        high_ref[0:rows, :] = high
        low_ref[0:rows, :] = low
        high_ref[rows : rows + edge, :] = jnp.zeros((edge, LANES), jnp.float32)
        low_ref[rows : rows + edge, :] = jnp.zeros((edge, LANES), jnp.float32)

    first = lane_index((blocks, LANES)) < HALF
    for p in range(0, SUB, 2):
        one, two = pl.ds(p, blocks, stride=SUB), pl.ds(p + 1, blocks, stride=SUB)
        even = jnp.where(first, x_ref[g, one, :], xr_ref[two, :])
        odd = jnp.where(first, xr_ref[one, :], x_ref[g, two, :])
        left = jnp.concatenate([even, odd, even, odd], axis=0).T
        left_high, left_low = split(left)
        left = jnp.concatenate([left_high, left_low[:, : 2 * blocks]], axis=1)
        for side in range(2):
            parts = []
            for ref in (eh, oh, el, ol):
                pieces = [
                    ref[pl.ds(p + side + SUB * o, blocks, stride=SUB), :].astype(jnp.bfloat16)
                    for o in range(shifts)
                ]
                parts.append(jnp.concatenate(pieces, axis=1))
            right = jnp.concatenate(parts + parts[:2], axis=0)
            grams = jnp.dot(
                left[side * HALF : (side + 1) * HALF], right, preferred_element_type=jnp.float32
            )
            total = grams[0:SUB]
            for a in range(1, HALF // SUB):
                piece = grams[a * SUB : (a + 1) * SUB]
                total = total + pltpu.roll(piece, width - a * SUB, 1)
            store_tiles(tot, p + side, total)
    result = strided_tiles(tot, 0)
    for s in range(1, SUB):
        result = result + pltpu.roll(strided_tiles(tot, s), width - s, 1)
    o_ref[g] = result[:, :L] * scale

    pieces = []
    for q in range(L // LANES):
        at = rows - L // LANES * SUB + q * SUB
        tile = x[at : at + SUB]
        for r in range(LANES // FINE):
            pieces.append(pltpu.roll(tile, LANES - r * FINE, 1) if r else tile)
    tail = jnp.concatenate(pieces, axis=0).T[:FINE] * scale
    member = lane_index(tail.shape) % SUB
    tail = jnp.concatenate([jnp.where(member == p, tail, 0.0) for p in range(SUB)], axis=0)
    th_ref[g], tl_ref[g] = split(tail)


def edge_kernel(h_ref, th_ref, tl_ref, m_ref, o_ref, tot):
    tiles = L // LANES
    steps = LANES // FINE
    lanes = lane_index((SUB, LANES))
    columns = lane_index((SUB, L))
    nothing = jnp.zeros((SUB, LANES), jnp.float32)
    for g in range(h_ref.shape[0]):
        halo = [h_ref[g, t * SUB : (t + 1) * SUB, :] for t in range(tiles)]
        shifted = {}
        for r in range(steps):
            if r == 0:
                moved = halo
            else:
                moved = [pltpu.roll(t, LANES - r * FINE, 1) for t in halo]
            for t in range(-1, tiles):
                if r == 0:
                    tile = moved[t] if t >= 0 else None
                else:
                    here = moved[t] if t >= 0 else nothing
                    after = moved[t + 1] if t + 1 < tiles else nothing
                    tile = jnp.where(lanes < LANES - r * FINE, here, after)
                shifted[r, t] = None if tile is None else split_wide(tile)
        packed = {}

        def both(b, column, which):
            key = []
            for at in (b, b + 1):
                q, r = divmod(at + 1, steps)
                tile = q + column - tiles
                key.append((r, tile) if shifted.get((r, tile)) is not None else None)
            key = (tuple(key), which)
            if key not in packed:
                rows = [nothing if k is None else shifted[k][which] for k in key[0]]
                packed[key] = jnp.concatenate(rows, axis=0).astype(jnp.bfloat16)
            return packed[key]

        right = []
        for which in range(2):
            right.append(
                jnp.concatenate(
                    [
                        jnp.concatenate([both(b, c, which) for c in range(tiles)], axis=1)
                        for b in range(0, L // FINE, 2)
                    ],
                    axis=0,
                )
            )
        left_high, left_low = th_ref[g], tl_ref[g]
        grams = (
            jnp.dot(left_high, right[0], preferred_element_type=jnp.float32)
            + jnp.dot(left_high, right[1], preferred_element_type=jnp.float32)
            + jnp.dot(left_low, right[0], preferred_element_type=jnp.float32)
        )
        for p in range(SUB):
            low_half = grams[p * FINE : p * FINE + SUB]
            high_half = grams[p * FINE + SUB : (p + 1) * FINE]
            moved = jnp.where(columns < SUB, 0.0, pltpu.roll(low_half, SUB, 1))
            store_tiles(tot, p, high_half + moved)
        result = m_ref[g]
        for s in range(SUB):
            moved = pltpu.roll(strided_tiles(tot, s), SUB - s, 1)
            result = result + jnp.where(columns < SUB - s, 0.0, moved)
        o_ref[g] = result


def tiles_of(array):
    pairs_here, length = array.shape
    groups, blocks = pairs_here // SUB, length // LANES
    tiles = array.reshape(groups, SUB, blocks, LANES).transpose(0, 2, 1, 3)
    return tiles.reshape(groups, blocks * SUB, LANES)


def vmem(count):
    return [pl.BlockSpec(memory_space=pltpu.VMEM)] * count


def load(x, y):
    head = (x.shape[0], L // LANES * SUB, LANES)
    return pl.pallas_call(
        load_kernel,
        name="load_part",
        in_specs=[pl.BlockSpec(memory_space=pltpu.HBM)] * 2,
        out_specs=vmem(3),
        out_shape=[jax.ShapeDtypeStruct(shape, jnp.float32) for shape in (x.shape, y.shape, head)],
        scratch_shapes=[pltpu.SemaphoreType.DMA((2,))],
        compiler_params=pltpu.CompilerParams(vmem_limit_bytes=4 << 20),
    )(*[pltpu.with_memory_space_constraint(v, pltpu.HBM) for v in (x, y)])


def main_products(x, y, scale):
    groups, rows, _ = x.shape
    shifts = L // LANES + 1
    tail_shape = jax.ShapeDtypeStruct((groups, SUB * FINE, SUB * L // FINE), jnp.bfloat16)
    wide = pltpu.VMEM((rows + (shifts - 1) * SUB, LANES), jnp.float32)
    return pl.pallas_call(
        lambda *refs: main_kernel(scale, *refs),
        name="main_part",
        in_specs=vmem(2),
        out_specs=vmem(3),
        out_shape=[jax.ShapeDtypeStruct((groups, SUB, L), jnp.float32), tail_shape, tail_shape],
        scratch_shapes=[pltpu.VMEM((rows, LANES), jnp.float32), wide, wide, wide, wide]
        + [pltpu.VMEM((shifts, SUB * SUB, LANES), jnp.float32)],
        compiler_params=pltpu.CompilerParams(vmem_limit_bytes=16 << 20),
        cost_estimate=pl.CostEstimate(
            flops=6 * groups * SUB * rows // SUB * LANES * L,
            bytes_accessed=8 * groups * rows * LANES,
            transcendentals=0,
        ),
    )(x, y)


def edge_products(halo, tail_high, tail_low, partial):
    return pl.pallas_call(
        edge_kernel,
        name="edge_part",
        in_specs=vmem(4),
        out_specs=vmem(1)[0],
        out_shape=jax.ShapeDtypeStruct(partial.shape, jnp.float32),
        scratch_shapes=[pltpu.VMEM((L // LANES, SUB * SUB, LANES), jnp.float32)],
        compiler_params=pltpu.CompilerParams(vmem_limit_bytes=8 << 20),
    )(halo, tail_high, tail_low, partial)


def body(x, y):
    tm, pair = lax.axis_size("tm"), lax.axis_size("pair")
    pairs_here, length = x.shape
    x_tiles, y_tiles, head = load(tiles_of(x), tiles_of(y))
    halo = lax.ppermute(head, "tm", [(i, i - 1) for i in range(1, tm)])
    scale = 1.0 / math.sqrt(tm * length)
    partial, tail_high, tail_low = main_products(x_tiles, y_tiles, scale)
    partial = edge_products(halo, tail_high, tail_low, partial)
    out_rows = pairs_here * pair // tm
    out_cols = L // pair
    blocks_here = pairs_here // out_rows
    mine = partial.reshape(blocks_here, out_rows, pair, out_cols).transpose(0, 2, 1, 3)
    send = jnp.zeros((tm, pair, out_rows, out_cols), jnp.float32)
    place = lax.axis_index("pair") * blocks_here
    send = lax.dynamic_update_slice(send, mine, (place, 0, 0, 0))
    send = send.reshape(tm * pair, out_rows, out_cols)
    received = lax.all_to_all(send, ("tm", "pair"), 0, 0, tiled=True)
    return jnp.sum(received, axis=0)


def solution(mesh):
    specs = (P("pair", "tm"), P("pair", "tm"))
    return jax.shard_map(
        body, mesh=mesh, in_specs=specs, out_specs=P("tm", "pair"), check_vma=False
    )
```

time: 36.8 us -> 28.6 us (0.78)
  waiting for transfers between devices: 5.84 us -> 0.43 us
  local copies, waits for them, and re-layouts: 2.36 us -> 0.06 us
  Pallas kernels: 9.8 us -> 7.51 us
  blocking collectives: 16.6 us -> 18.4 us
    ppermute x1, waiting for transfers between devices: 5.84 us -> 0.43 us  [body(): halo = lax.ppermute(head, 'tm', [(i, i - 1) for i in range(1, tm)])]
    pallas_call x1 -> x3, Pallas kernels: 9.8 us -> 7.51 us  [the longest x1 5.4 us: main_products(): pl.pallas_call(lambda *refs: main_kernel(scale, *refs), name='main_part',...]
    all_to_all x1, blocking collectives: 16.6 us -> 18.4 us  [body(): received = lax.all_to_all(send, ('tm', 'pair'), 0, 0, tiled=True)]
    slice x1 -> x0, local copies, waits for them, and re-layouts: 0.84 us -> none  [body(): halo = lax.ppermute(y[:, :L], 'tm', [(i, i - 1) for i in range(1, tm)])]
    reshape x1, local copies, waits for them, and re-layouts: 0.86 us -> 0.02 us  [body(): partial.reshape(blocks_here, out_rows, pair, out_cols).transpose(0, 2, 1, 3)]
    unnamed x2 -> x0, local copies, waits for them, and re-layouts: 0.62 us -> none
    mul x1 -> x0, other arithmetic: 0.6 us -> none  [body(): return jnp.sum(received, axis=0) * (1.0 / math.sqrt(tm * length))]
    reduce_sum x1, other arithmetic: 0.04 us -> 0.63 us  [body(): return jnp.sum(received, axis=0)]
  transfers between devices with their start and end apart: 1 -> 1, of which waited for: 1 -> 1; matrix products, arithmetic and copies ran while one was open for 0% -> 0% of each run, Pallas kernels for 0% -> 19%
where the time goes in v2:
time: 28.6 us; the launch traced here: 28.4 us
  blocking collectives  18.4 us (64%)
  Pallas kernels  7.51 us (26%)
  starting transfers between devices  1.29 us (5%)
  other arithmetic  0.63 us (2%)
  waiting for transfers between devices  0.43 us (2%)
    all_to_all x1, blocking collectives, body(): received = lax.all_to_all(send, ('tm', 'pair'), 0, 0, tiled=True)  18.4 us
    pallas_call x1, Pallas kernels, main_products(): pl.pallas_call(lambda *refs: main_kernel(scale, *refs), name='main_part',...  5.4 us
    ppermute x1, starting transfers between devices, body(): halo = lax.ppermute(head, 'tm', [(i, i - 1) for i in range(1, tm)])  1.29 us
    pallas_call x1, Pallas kernels, load(): pl.pallas_call(load_kernel, name='load_part', in_specs=[pl.BlockSpec(memo...  1.22 us
    pallas_call x1, Pallas kernels, edge_products(): pl.pallas_call(edge_kernel, name='edge_part', in_specs=vmem(4), out_specs...  0.9 us
    reduce_sum x1, other arithmetic, body(): return jnp.sum(received, axis=0)  0.63 us
  transfers between devices with their start and end apart: 1, of which 1 were waited for; matrix products, arithmetic and copies ran while one was open for 0% of the time, Pallas kernels for 19%

profile of v2, /device:TPU:0, one launch (start us, length us, event | category | flops | bytes accessed | tf_op | source)
XLA Modules:
  0.0 28.4 jit_solution(2441392395308271825)
XLA Ops:
  0.0 1.2 %load_part.1 = (f32[4,256,128]{2,1,0:T(8,128)S(1)}, f32[4,256,128]{2,1,0:T(8,128)S(1)}, f32[4,32,128]{2,1,0:T(8,128)S(1)}) custom-call(f32[4,256,128]{2,1,0:T(8,128)} %bitcast.14, f32[4,256,128]{2,1,0:T(8,128)} %bitcast.15), custom_call_target="tpu_custom_call" | custom-call | tf_op jit(solution)/shard_map/load_part/pallas_call | solution.py:199
  1.2 1.3 %collective-permute-start = (f32[4,32,128]{2,1,0:T(8,128)S(1)}, f32[4,32,128]{2,1,0:T(8,128)S(1)}, u32[]{:S(2)}, u32[]{:S(2)}) collective-permute-start(f32[4,32,128]{2,1,0:T(8,128)S(1)} %get-tuple-element.11), channel_id=1, source_target_pairs={{4,0},{8,4},{12,8},{16,12},{20,16},{24,20},{28,24},{5,1},{9,5},{13... | collective-permute-start | bytes 196616 | tf_op jit(solution)/shard_map/ppermute | solution.py:248
  2.5 5.4 %main_part.1 = (f32[4,8,512]{2,1,0:T(8,128)S(1)}, bf16[4,128,256]{2,1,0:T(8,128)(2,1)S(1)}, bf16[4,128,256]{2,1,0:T(8,128)(2,1)S(1)}) custom-call(f32[4,256,128]{2,1,0:T(8,128)S(1)} %get-tuple-element.12.refs_0_, f32[4,256,128]{2,1,0:T(8,128)S(1)} %get-tuple-element.13.refs_1_), custom_call_target="tpu_custom_call" | custom-call | flops 402653184 | bytes 1048576 | tf_op jit(solution)/shard_map/main_part/pallas_call | solution.py:215
  7.9 0.4 %collective-permute-done.h_ref = f32[4,32,128]{2,1,0:T(8,128)S(1)} collective-permute-done((f32[4,32,128]{2,1,0:T(8,128)S(1)}, f32[4,32,128]{2,1,0:T(8,128)S(1)}, u32[]{:S(2)}, u32[]{:S(2)}) %collective-permute-start) | collective-permute-done | bytes 65568 | tf_op jit(solution)/shard_map/ppermute | solution.py:248
  8.4 0.9 %edge_part.1 = f32[4,8,512]{2,1,0:T(8,128)S(1)} custom-call(f32[4,32,128]{2,1,0:T(8,128)S(1)} %collective-permute-done.h_ref, bf16[4,128,256]{2,1,0:T(8,128)(2,1)S(1)} %get-tuple-element.14.th_ref, bf16[4,128,256]{2,1,0:T(8,128)(2,1)S(1)} %get-tuple-element.15.tl_ref, f32[4,8,512]{2,1,0:T(8,128)S(1)} %get-tuple-element.16.m_ref), custom_call_target="tpu_custom_call" | custom-call | tf_op jit(solution)/shard_map/edge_part/pallas_call | solution.py:233
  9.3 18.4 %all_to_all.5 = f32[32,16,128]{2,1,0:T(8,128)S(1)} all-to-all(f32[32,16,128]{2,1,0:T(8,128)S(1)} %bitcast.13), channel_id=1, replica_groups=mesh['tm'=8,'pair'=4] {'tm','pair'}, dimensions={0} | all-to-all | bytes 524288 | tf_op jit(solution)/shard_map/all_to_all | solution.py:260
  27.8 0.6 %reduce_sum.9 = f32[16,128]{1,0:T(8,128)} reduce(f32[32,16,128]{2,1,0:T(8,128)S(1)} %all_to_all.5, f32[]{:T(128)} %constant.5.clone.1), dimensions={0}, to_apply=%region_0.0 | reduce | flops 63488 | bytes 270340 | tf_op jit(solution)/shard_map/reduce_sum | solution.py:261
  (3 shorter events, 0.1 us)
Async XLA Ops:
  1.2 7.1 %collective-permute-start = (f32[4,32,128]{2,1,0:T(8,128)S(1)}, f32[4,32,128]{2,1,0:T(8,128)S(1)}, u32[]{:S(2)}, u32[]{:S(2)}) collective-permute-start(f32[4,32,128]{2,1,0:T(8,128)S(1)} %get-tuple-element.11), channel_id=1, source_target_pairs={{4,0},{8,4},{12,8},{16,12},{20,16},{24,20},{28,24},{5,1},{9,5},{13... | collective-permute-start | bytes 196616 | tf_op jit(solution)/shard_map/ppermute | solution.py:248

commit v3 on v2

--- a/solution.py
+++ b/solution.py
@@ -10,6 +10,7 @@
 L = 512
 LANES = 128
 SUB = 8
+PITCH = SUB + 1
 HALF = LANES // 2
 FINE = 16
 
@@ -30,11 +31,11 @@
 
 def store_tiles(ref, p, value):
     for o in range(ref.shape[0]):
-        ref[o, p * SUB : (p + 1) * SUB, :] = value[:, o * LANES : (o + 1) * LANES]
+        ref[o, p * PITCH : p * PITCH + SUB, :] = value[:, o * LANES : (o + 1) * LANES]
 
 
 def strided_tiles(ref, s):
-    at = pl.ds(s, SUB, stride=SUB)
+    at = pl.ds(s, SUB, stride=PITCH)
     return jnp.concatenate([ref[o, at, :] for o in range(ref.shape[0])], axis=1)
 
 
@@ -48,74 +49,146 @@
     fetch_x.wait()
 
 
-def main_kernel(scale, x_ref, y_ref, o_ref, th_ref, tl_ref, *scratch):
-    def step(g, carry):
-        main_group(g, scale, x_ref, y_ref, o_ref, th_ref, tl_ref, *scratch)
-        return carry
-
-    lax.fori_loop(0, x_ref.shape[0], step, 0)
-
-
-def main_group(g, scale, x_ref, y_ref, o_ref, th_ref, tl_ref, xr_ref, eh, el, oh, ol, tot):
-    rows = y_ref.shape[1]
-    blocks = rows // SUB
+def turned(eye, value):
+    dims = (((1,), (1,)), ((), ()))
+    out = lax.dot_general(eye, value, dims, preferred_element_type=jnp.float32)
+    return out.astype(jnp.bfloat16)
+
+
+def identity(rows):
+    shape = (rows, LANES)
+    same = lax.broadcasted_iota(jnp.int32, shape, 0) == lane_index(shape)
+    return jnp.where(same, 1.0, 0.0).astype(jnp.bfloat16)
+
+
+def spread(ref, value):
+    for b in range(value.shape[0] // SUB):
+        ref[b * PITCH : b * PITCH + SUB, :] = value[b * SUB : (b + 1) * SUB]
+
+
+def packed(value, strips, shifts):
+    count = strips + shifts - 1
+    high, wide, low = {}, {}, {}
+    for j in range(0, count, 2):
+        high[j] = jnp.concatenate(value[j : j + 2], axis=0).astype(jnp.bfloat16)
+        back = high[j].astype(jnp.float32)
+        for k in range(2):
+            wide[j + k] = value[j + k] - back[k * SUB : (k + 1) * SUB]
+    for j in range(count - 1):
+        if j not in high:
+            high[j] = jnp.concatenate(value[j : j + 2], axis=0).astype(jnp.bfloat16)
+        low[j] = jnp.concatenate([wide[j], wide[j + 1]], axis=0).astype(jnp.bfloat16)
+    tiles = []
+    for part in (high, low):
+        columns = [
+            jnp.concatenate([part[o + j] for j in range(0, strips, 2)], axis=0)
+            for o in range(shifts)
+        ]
+        tiles.append(jnp.concatenate(columns, axis=1))
+    return tiles
+
+
+def main_kernel(scale, x_ref, y_ref, o_ref, th_ref, tl_ref, xe_ref, xo_ref, ye_ref, yo_ref, tot):
+    groups, rows, _ = y_ref.shape
+    depth = xe_ref.shape[0]
+    strips = rows // SUB // SUB
     shifts = L // LANES + 1
     width = shifts * LANES
-    edge = (shifts - 1) * SUB
-    x = x_ref[g]
-    xr_ref[...] = pltpu.roll(x, HALF, 1)
-    y = y_ref[g]
-    y_rolled = pltpu.roll(y, HALF, 1)
-    nothing = jnp.zeros((SUB, LANES), jnp.float32)
-    y_next = jnp.concatenate([y_rolled[SUB:], nothing], axis=0)
-    y_odd = jnp.where(lane_index(y.shape) < HALF, y_rolled, y_next)
-    for value, high_ref, low_ref in ((y, eh, el), (y_odd, oh, ol)):
-        high, low = split_wide(value)
-        high_ref[0:rows, :] = high
-        low_ref[0:rows, :] = low
-        high_ref[rows : rows + edge, :] = jnp.zeros((edge, LANES), jnp.float32)
-        low_ref[rows : rows + edge, :] = jnp.zeros((edge, LANES), jnp.float32)
-
-    first = lane_index((blocks, LANES)) < HALF
-    for p in range(0, SUB, 2):
-        one, two = pl.ds(p, blocks, stride=SUB), pl.ds(p + 1, blocks, stride=SUB)
-        even = jnp.where(first, x_ref[g, one, :], xr_ref[two, :])
-        odd = jnp.where(first, xr_ref[one, :], x_ref[g, two, :])
-        left = jnp.concatenate([even, odd, even, odd], axis=0).T
-        left_high, left_low = split(left)
-        left = jnp.concatenate([left_high, left_low[:, : 2 * blocks]], axis=1)
+    eye, small_eye = identity(LANES), identity(FINE)
+    first = lane_index((SUB, LANES)) < HALF
+    for ref in (ye_ref, yo_ref):
+        used = rows // SUB * PITCH
+        for d in range(depth):
+            ref[d, used:, :] = jnp.zeros((ref.shape[1] - used, LANES), jnp.float32)
+
+    def strip(p, j):
+        return pl.ds(j * PITCH + p, SUB, stride=strips * PITCH)
+
+    def stage(g):
+        d = g % depth
+        x, y = x_ref[g], y_ref[g]
+        spread(xe_ref.at[d], x)
+        spread(xo_ref.at[d], pltpu.roll(x, HALF, 1))
+        spread(ye_ref.at[d], y)
+        y_rolled = pltpu.roll(y, HALF, 1)
+        nothing = jnp.zeros((SUB, LANES), jnp.float32)
+        y_next = jnp.concatenate([y_rolled[SUB:], nothing], axis=0)
+        spread(yo_ref.at[d], jnp.where(lane_index(y.shape) < HALF, y_rolled, y_next))
+
+    def turn(couple):
+        g, p = divmod(2 * couple, SUB)
+        d = g % depth
+        evens, odds = [], []
+        for j in range(strips):
+            one, two = strip(p, j), strip(p + 1, j)
+            evens.append(jnp.where(first, xe_ref[d, one, :], xo_ref[d, two, :]))
+            odds.append(jnp.where(first, xo_ref[d, one, :], xe_ref[d, two, :]))
+        high, low = split(jnp.concatenate(evens + odds, axis=0))
+        return turned(eye, jnp.concatenate([high, high, low], axis=0))
+
+    def multiply(couple, left, side):
+        g, p = divmod(2 * couple + side, SUB)
+        d = g % depth
+        count = strips + shifts - 1
+        even = packed([ye_ref[d, strip(p, j), :] for j in range(count)], strips, shifts)
+        odd = packed([yo_ref[d, strip(p, j), :] for j in range(count)], strips, shifts)
+        right = jnp.concatenate([even[0], odd[0], even[1], odd[1], even[0], odd[0]], axis=0)
+        left = left[side * HALF : (side + 1) * HALF]
+        return jnp.dot(left, right, preferred_element_type=jnp.float32)
+
+    def fold(couple, grams, side):
+        g, p = divmod(2 * couple + side, SUB)
+        total = grams[0:SUB]
+        for a in range(1, HALF // SUB):
+            piece = grams[a * SUB : (a + 1) * SUB]
+            total = total + pltpu.roll(piece, width - a * SUB, 1)
+        store_tiles(tot.at[g % depth], p, total)
+
+    def finish(g):
+        own = tot.at[g % depth]
+        result = strided_tiles(own, 0)
+        for s in range(1, SUB):
+            result = result + pltpu.roll(strided_tiles(own, s), width - s, 1)
+        o_ref[g] = result[:, :L] * scale
+
+    def tail(g):
+        pieces = []
+        for q in range(L // LANES):
+            at = rows - L // LANES * SUB + q * SUB
+            tile = x_ref[g, at : at + SUB, :] * scale
+            for r in range(LANES // FINE):
+                pieces.append(pltpu.roll(tile, LANES - r * FINE, 1) if r else tile)
+        parts = split(jnp.concatenate(pieces, axis=0))
+        for part, ref in zip(parts, (th_ref, tl_ref)):
+            value = turned(small_eye, part)
+            member = lane_index(value.shape) % SUB
+            none = jnp.zeros_like(value)
+            ref[g] = jnp.concatenate(
+                [jnp.where(member == p, value, none) for p in range(SUB)], axis=0
+            )
+
+    per_group = SUB // 2
+    couples = groups * per_group
+    stage(0)
+    lefts = {0: turn(0)}
+    grams = {}
+    for k in range(couples + 1):
+        g, at = divmod(k, per_group)
+        if k < couples:
+            if at == 0:
+                tail(g)
+            if at == 1 and g + 1 < groups:
+                stage(g + 1)
+            if k + 1 < couples:
+                lefts[k + 1] = turn(k + 1)
+            left = lefts.pop(k)
         for side in range(2):
-            parts = []
-            for ref in (eh, oh, el, ol):
-                pieces = [
-                    ref[pl.ds(p + side + SUB * o, blocks, stride=SUB), :].astype(jnp.bfloat16)
-                    for o in range(shifts)
-                ]
-                parts.append(jnp.concatenate(pieces, axis=1))
-            right = jnp.concatenate(parts + parts[:2], axis=0)
-            grams = jnp.dot(
-                left[side * HALF : (side + 1) * HALF], right, preferred_element_type=jnp.float32
-            )
-            total = grams[0:SUB]
-            for a in range(1, HALF // SUB):
-                piece = grams[a * SUB : (a + 1) * SUB]
-                total = total + pltpu.roll(piece, width - a * SUB, 1)
-            store_tiles(tot, p + side, total)
-    result = strided_tiles(tot, 0)
-    for s in range(1, SUB):
-        result = result + pltpu.roll(strided_tiles(tot, s), width - s, 1)
-    o_ref[g] = result[:, :L] * scale
-
-    pieces = []
-    for q in range(L // LANES):
-        at = rows - L // LANES * SUB + q * SUB
-        tile = x[at : at + SUB]
-        for r in range(LANES // FINE):
-            pieces.append(pltpu.roll(tile, LANES - r * FINE, 1) if r else tile)
-    tail = jnp.concatenate(pieces, axis=0).T[:FINE] * scale
-    member = lane_index(tail.shape) % SUB
-    tail = jnp.concatenate([jnp.where(member == p, tail, 0.0) for p in range(SUB)], axis=0)
-    th_ref[g], tl_ref[g] = split(tail)
+            if k < couples:
+                grams[k, side] = multiply(k, left, side)
+            if k > 0:
+                fold(k - 1, grams.pop((k - 1, side)), side)
+        if k > 0 and at == 0:
+            finish(g - 1)
 
 
 def edge_kernel(h_ref, th_ref, tl_ref, m_ref, o_ref, tot):
@@ -211,15 +284,16 @@
     groups, rows, _ = x.shape
     shifts = L // LANES + 1
     tail_shape = jax.ShapeDtypeStruct((groups, SUB * FINE, SUB * L // FINE), jnp.bfloat16)
-    wide = pltpu.VMEM((rows + (shifts - 1) * SUB, LANES), jnp.float32)
+    narrow = pltpu.VMEM((2, rows // SUB * PITCH, LANES), jnp.float32)
+    wide = pltpu.VMEM((2, (rows // SUB + shifts - 1) * PITCH, LANES), jnp.float32)
     return pl.pallas_call(
         lambda *refs: main_kernel(scale, *refs),
         name="main_part",
         in_specs=vmem(2),
         out_specs=vmem(3),
         out_shape=[jax.ShapeDtypeStruct((groups, SUB, L), jnp.float32), tail_shape, tail_shape],
-        scratch_shapes=[pltpu.VMEM((rows, LANES), jnp.float32), wide, wide, wide, wide]
-        + [pltpu.VMEM((shifts, SUB * SUB, LANES), jnp.float32)],
+        scratch_shapes=[narrow, narrow, wide, wide]
+        + [pltpu.VMEM((2, shifts, SUB * PITCH, LANES), jnp.float32)],
         compiler_params=pltpu.CompilerParams(vmem_limit_bytes=16 << 20),
         cost_estimate=pl.CostEstimate(
             flops=6 * groups * SUB * rows // SUB * LANES * L,
@@ -236,7 +310,7 @@
         in_specs=vmem(4),
         out_specs=vmem(1)[0],
         out_shape=jax.ShapeDtypeStruct(partial.shape, jnp.float32),
-        scratch_shapes=[pltpu.VMEM((L // LANES, SUB * SUB, LANES), jnp.float32)],
+        scratch_shapes=[pltpu.VMEM((L // LANES, SUB * PITCH, LANES), jnp.float32)],
         compiler_params=pltpu.CompilerParams(vmem_limit_bytes=8 << 20),
     )(halo, tail_high, tail_low, partial)
 

time: 28.6 us -> 26.8 us (0.937)
  Pallas kernels: 7.51 us -> 4.93 us
  waiting for transfers between devices: 0.43 us -> 3.01 us
  blocking collectives: 18.4 us -> 16.6 us
    ppermute x1, waiting for transfers between devices: 0.43 us -> 3.01 us  [body(): halo = lax.ppermute(head, 'tm', [(i, i - 1) for i in range(1, tm)])]
    pallas_call x1, Pallas kernels: 5.4 us -> 2.82 us  [main_products(): pl.pallas_call(lambda *refs: main_kernel(scale, *refs), name='main_part',...]
    all_to_all x1, blocking collectives: 18.4 us -> 16.6 us  [body(): received = lax.all_to_all(send, ('tm', 'pair'), 0, 0, tiled=True)]
  transfers between devices with their start and end apart: 1 -> 1, of which waited for: 1 -> 1; matrix products, arithmetic and copies ran while one was open for 0% -> 0% of each run, Pallas kernels for 19% -> 11%
where the time goes in v3:
time: 26.8 us; the launch traced here: 26.6 us
  blocking collectives  16.6 us (62%)
  Pallas kernels  4.93 us (18%)
  waiting for transfers between devices  3.01 us (11%)
  starting transfers between devices  1.29 us (5%)
  other arithmetic  0.63 us (2%)
    all_to_all x1, blocking collectives, body(): received = lax.all_to_all(send, ('tm', 'pair'), 0, 0, tiled=True)  16.6 us
    ppermute x1, waiting for transfers between devices, body(): halo = lax.ppermute(head, 'tm', [(i, i - 1) for i in range(1, tm)])  3.01 us
    pallas_call x1, Pallas kernels, main_products(): pl.pallas_call(lambda *refs: main_kernel(scale, *refs), name='main_part',...  2.82 us
    ppermute x1, starting transfers between devices, body(): halo = lax.ppermute(head, 'tm', [(i, i - 1) for i in range(1, tm)])  1.29 us
    pallas_call x1, Pallas kernels, load(): pl.pallas_call(load_kernel, name='load_part', in_specs=[pl.BlockSpec(memo...  1.22 us
    pallas_call x1, Pallas kernels, edge_products(): pl.pallas_call(edge_kernel, name='edge_part', in_specs=vmem(4), out_specs...  0.89 us
    reduce_sum x1, other arithmetic, body(): return jnp.sum(received, axis=0)  0.63 us
  transfers between devices with their start and end apart: 1, of which 1 were waited for; matrix products, arithmetic and copies ran while one was open for 0% of the time, Pallas kernels for 11%

profile of v3, /device:TPU:0, one launch (start us, length us, event | category | flops | bytes accessed | tf_op | source)
XLA Modules:
  0.0 26.6 jit_solution(9183771329738086630)
XLA Ops:
  0.0 1.2 %load_part.1 = (f32[4,256,128]{2,1,0:T(8,128)S(1)}, f32[4,256,128]{2,1,0:T(8,128)S(1)}, f32[4,32,128]{2,1,0:T(8,128)S(1)}) custom-call(f32[4,256,128]{2,1,0:T(8,128)} %bitcast.14, f32[4,256,128]{2,1,0:T(8,128)} %bitcast.15), custom_call_target="tpu_custom_call" | custom-call | tf_op jit(solution)/shard_map/load_part/pallas_call | solution.py:272
  1.2 1.3 %collective-permute-start = (f32[4,32,128]{2,1,0:T(8,128)S(1)}, f32[4,32,128]{2,1,0:T(8,128)S(1)}, u32[]{:S(2)}, u32[]{:S(2)}) collective-permute-start(f32[4,32,128]{2,1,0:T(8,128)S(1)} %get-tuple-element.11), channel_id=1, source_target_pairs={{4,0},{8,4},{12,8},{16,12},{20,16},{24,20},{28,24},{5,1},{9,5},{13... | collective-permute-start | bytes 196616 | tf_op jit(solution)/shard_map/ppermute | solution.py:322
  2.5 2.8 %main_part.1 = (f32[4,8,512]{2,1,0:T(8,128)S(1)}, bf16[4,128,256]{2,1,0:T(8,128)(2,1)S(1)}, bf16[4,128,256]{2,1,0:T(8,128)(2,1)S(1)}) custom-call(f32[4,256,128]{2,1,0:T(8,128)S(1)} %get-tuple-element.12.refs_0_, f32[4,256,128]{2,1,0:T(8,128)S(1)} %get-tuple-element.13.refs_1_), custom_call_target="tpu_custom_call" | custom-call | flops 402653184 | bytes 1048576 | tf_op jit(solution)/shard_map/main_part/pallas_call | solution.py:289
  5.4 3.0 %collective-permute-done.h_ref = f32[4,32,128]{2,1,0:T(8,128)S(1)} collective-permute-done((f32[4,32,128]{2,1,0:T(8,128)S(1)}, f32[4,32,128]{2,1,0:T(8,128)S(1)}, u32[]{:S(2)}, u32[]{:S(2)}) %collective-permute-start) | collective-permute-done | bytes 65568 | tf_op jit(solution)/shard_map/ppermute | solution.py:322
  8.4 0.9 %edge_part.1 = f32[4,8,512]{2,1,0:T(8,128)S(1)} custom-call(f32[4,32,128]{2,1,0:T(8,128)S(1)} %collective-permute-done.h_ref, bf16[4,128,256]{2,1,0:T(8,128)(2,1)S(1)} %get-tuple-element.14.th_ref, bf16[4,128,256]{2,1,0:T(8,128)(2,1)S(1)} %get-tuple-element.15.tl_ref, f32[4,8,512]{2,1,0:T(8,128)S(1)} %get-tuple-element.16.m_ref), custom_call_target="tpu_custom_call" | custom-call | tf_op jit(solution)/shard_map/edge_part/pallas_call | solution.py:307
  9.3 16.6 %all_to_all.5 = f32[32,16,128]{2,1,0:T(8,128)S(1)} all-to-all(f32[32,16,128]{2,1,0:T(8,128)S(1)} %bitcast.13), channel_id=1, replica_groups=mesh['tm'=8,'pair'=4] {'tm','pair'}, dimensions={0} | all-to-all | bytes 524288 | tf_op jit(solution)/shard_map/all_to_all | solution.py:334
  26.0 0.6 %reduce_sum.9 = f32[16,128]{1,0:T(8,128)} reduce(f32[32,16,128]{2,1,0:T(8,128)S(1)} %all_to_all.5, f32[]{:T(128)} %constant.5.clone.1), dimensions={0}, to_apply=%region_0.0 | reduce | flops 63488 | bytes 270340 | tf_op jit(solution)/shard_map/reduce_sum | solution.py:335
  (3 shorter events, 0.1 us)
Async XLA Ops:
  1.2 7.1 %collective-permute-start = (f32[4,32,128]{2,1,0:T(8,128)S(1)}, f32[4,32,128]{2,1,0:T(8,128)S(1)}, u32[]{:S(2)}, u32[]{:S(2)}) collective-permute-start(f32[4,32,128]{2,1,0:T(8,128)S(1)} %get-tuple-element.11), channel_id=1, source_target_pairs={{4,0},{8,4},{12,8},{16,12},{20,16},{24,20},{28,24},{5,1},{9,5},{13... | collective-permute-start | bytes 196616 | tf_op jit(solution)/shard_map/ppermute | solution.py:322

commit v4 on v3

--- a/solution.py
+++ b/solution.py
@@ -13,6 +13,7 @@
 PITCH = SUB + 1
 HALF = LANES // 2
 FINE = 16
+FLOPS = 10000000000
 
 
 def split(value):
@@ -27,6 +28,22 @@
 
 def lane_index(shape):
     return lax.broadcasted_iota(jnp.int32, shape, 1)
+
+
+def store_tiles(ref, p, value):
+    for o in range(ref.shape[0]):
+        ref[o, p * PITCH : p * PITCH + SUB, :] = value[:, o * LANES : (o + 1) * LANES]
+
+
+def strided_tiles(ref, s):
+    at = pl.ds(s, SUB, stride=PITCH)
+    return jnp.concatenate([ref[o, at, :] for o in range(ref.shape[0])], axis=1)
+
+
+def head_kernel(y_hbm, head_ref, sem):
+    copy = pltpu.make_async_copy(y_hbm.at[:, : head_ref.shape[1], :], head_ref, sem)
+    copy.start()
+    copy.wait()
 
 
 def store_tiles(ref, p, value):
@@ -197,63 +214,75 @@
     lanes = lane_index((SUB, LANES))
     columns = lane_index((SUB, L))
     nothing = jnp.zeros((SUB, LANES), jnp.float32)
-    for g in range(h_ref.shape[0]):
+    groups = h_ref.shape[0]
+    fine_blocks = L // FINE
+
+    def shifted_halo(g):
         halo = [h_ref[g, t * SUB : (t + 1) * SUB, :] for t in range(tiles)]
         shifted = {}
         for r in range(steps):
-            if r == 0:
-                moved = halo
-            else:
-                moved = [pltpu.roll(t, LANES - r * FINE, 1) for t in halo]
-            for t in range(-1, tiles):
-                if r == 0:
-                    tile = moved[t] if t >= 0 else None
-                else:
+            moved = [pltpu.roll(t, LANES - r * FINE, 1) if r else t for t in halo]
+            for t in range(-1 if r else 0, tiles):
+                tile = moved[max(t, 0)]
+                if r:
                     here = moved[t] if t >= 0 else nothing
                     after = moved[t + 1] if t + 1 < tiles else nothing
                     tile = jnp.where(lanes < LANES - r * FINE, here, after)
-                shifted[r, t] = None if tile is None else split_wide(tile)
-        packed = {}
-
-        def both(b, column, which):
+                shifted[r, t] = split_wide(tile)
+        return shifted
+
+    def right_side(shifted, which):
+        made = {}
+
+        def piece(b, column):
             key = []
             for at in (b, b + 1):
                 q, r = divmod(at + 1, steps)
-                tile = q + column - tiles
-                key.append((r, tile) if shifted.get((r, tile)) is not None else None)
-            key = (tuple(key), which)
-            if key not in packed:
-                rows = [nothing if k is None else shifted[k][which] for k in key[0]]
-                packed[key] = jnp.concatenate(rows, axis=0).astype(jnp.bfloat16)
-            return packed[key]
-
-        right = []
-        for which in range(2):
-            right.append(
-                jnp.concatenate(
-                    [
-                        jnp.concatenate([both(b, c, which) for c in range(tiles)], axis=1)
-                        for b in range(0, L // FINE, 2)
-                    ],
-                    axis=0,
-                )
-            )
+                key.append((r, q + column - tiles))
+            key = tuple(k if k in shifted else None for k in key)
+            if key not in made:
+                rows = [nothing if k is None else shifted[k][which] for k in key]
+                made[key] = jnp.concatenate(rows, axis=0).astype(jnp.bfloat16)
+            return made[key]
+
+        rows = [
+            jnp.concatenate([piece(b, c) for c in range(tiles)], axis=1)
+            for b in range(0, fine_blocks, 2)
+        ]
+        return jnp.concatenate(rows, axis=0)
+
+    def multiply(g):
+        shifted = shifted_halo(g)
+        right_high, right_low = right_side(shifted, 0), right_side(shifted, 1)
         left_high, left_low = th_ref[g], tl_ref[g]
-        grams = (
-            jnp.dot(left_high, right[0], preferred_element_type=jnp.float32)
-            + jnp.dot(left_high, right[1], preferred_element_type=jnp.float32)
-            + jnp.dot(left_low, right[0], preferred_element_type=jnp.float32)
-        )
+        half = tiles // 2
+        parts = []
+        for first, at in ((half * steps, slice(0, half * LANES)), (0, slice(half * LANES, L))):
+            k = slice(first * SUB, fine_blocks * SUB)
+            high, low = right_high[k, at], right_low[k, at]
+            left = jnp.concatenate([left_high[:, k], left_high[:, k], left_low[:, k]], axis=1)
+            right = jnp.concatenate([high, low, high], axis=0)
+            parts.append(jnp.dot(left, right, preferred_element_type=jnp.float32))
+        return jnp.concatenate(parts, axis=1)
+
+    def fold(g, grams):
+        own = tot.at[g % 2]
         for p in range(SUB):
             low_half = grams[p * FINE : p * FINE + SUB]
             high_half = grams[p * FINE + SUB : (p + 1) * FINE]
             moved = jnp.where(columns < SUB, 0.0, pltpu.roll(low_half, SUB, 1))
-            store_tiles(tot, p, high_half + moved)
+            store_tiles(own, p, high_half + moved)
         result = m_ref[g]
         for s in range(SUB):
-            moved = pltpu.roll(strided_tiles(tot, s), SUB - s, 1)
+            moved = pltpu.roll(strided_tiles(own, s), SUB - s, 1)
             result = result + jnp.where(columns < SUB - s, 0.0, moved)
         o_ref[g] = result
+
+    grams = multiply(0)
+    for g in range(groups):
+        after = multiply(g + 1) if g + 1 < groups else None
+        fold(g, grams)
+        grams = after
 
 
 def tiles_of(array):
@@ -267,17 +296,18 @@
     return [pl.BlockSpec(memory_space=pltpu.VMEM)] * count
 
 
-def load(x, y):
-    head = (x.shape[0], L // LANES * SUB, LANES)
+def head_of(y):
+    head = (y.shape[0], L // LANES * SUB, LANES)
     return pl.pallas_call(
-        load_kernel,
-        name="load_part",
-        in_specs=[pl.BlockSpec(memory_space=pltpu.HBM)] * 2,
-        out_specs=vmem(3),
-        out_shape=[jax.ShapeDtypeStruct(shape, jnp.float32) for shape in (x.shape, y.shape, head)],
-        scratch_shapes=[pltpu.SemaphoreType.DMA((2,))],
+        head_kernel,
+        name="head_part",
+        in_specs=[pl.BlockSpec(memory_space=pltpu.HBM)],
+        out_specs=vmem(1)[0],
+        out_shape=jax.ShapeDtypeStruct(head, jnp.float32),
+        scratch_shapes=[pltpu.SemaphoreType.DMA],
         compiler_params=pltpu.CompilerParams(vmem_limit_bytes=4 << 20),
-    )(*[pltpu.with_memory_space_constraint(v, pltpu.HBM) for v in (x, y)])
+        cost_estimate=pl.CostEstimate(flops=FLOPS, bytes_accessed=0, transcendentals=0),
+    )(pltpu.with_memory_space_constraint(y, pltpu.HBM))
 
 
 def main_products(x, y, scale):
@@ -310,7 +340,7 @@
         in_specs=vmem(4),
         out_specs=vmem(1)[0],
         out_shape=jax.ShapeDtypeStruct(partial.shape, jnp.float32),
-        scratch_shapes=[pltpu.VMEM((L // LANES, SUB * PITCH, LANES), jnp.float32)],
+        scratch_shapes=[pltpu.VMEM((2, L // LANES, SUB * PITCH, LANES), jnp.float32)],
         compiler_params=pltpu.CompilerParams(vmem_limit_bytes=8 << 20),
     )(halo, tail_high, tail_low, partial)
 
@@ -318,8 +348,8 @@
 def body(x, y):
     tm, pair = lax.axis_size("tm"), lax.axis_size("pair")
     pairs_here, length = x.shape
-    x_tiles, y_tiles, head = load(tiles_of(x), tiles_of(y))
-    halo = lax.ppermute(head, "tm", [(i, i - 1) for i in range(1, tm)])
+    x_tiles, y_tiles = tiles_of(x), tiles_of(y)
+    halo = lax.ppermute(head_of(y_tiles), "tm", [(i, i - 1) for i in range(1, tm)])
     scale = 1.0 / math.sqrt(tm * length)
     partial, tail_high, tail_low = main_products(x_tiles, y_tiles, scale)
     partial = edge_products(halo, tail_high, tail_low, partial)

time: 26.8 us -> 26.4 us (0.985)
  Pallas kernels: 4.93 us -> 4.57 us
    pallas_call x1, Pallas kernels: 1.22 us -> 0.94 us  [head_of(): pl.pallas_call(head_kernel, name='head_part', in_specs=[pl.BlockSpec(memo...]
where the time goes in v4:
time: 26.4 us; the launch traced here: 26.2 us
  blocking collectives  16.6 us (63%)
  Pallas kernels  4.57 us (17%)
  waiting for transfers between devices  2.99 us (11%)
  starting transfers between devices  1.29 us (5%)
  other arithmetic  0.63 us (2%)
    all_to_all x1, blocking collectives, body(): received = lax.all_to_all(send, ('tm', 'pair'), 0, 0, tiled=True)  16.6 us
    ppermute x1, waiting for transfers between devices, body(): lax.ppermute(head_of(y_tiles), 'tm', [(i, i - 1) for i in range(1, tm)])  2.99 us
    pallas_call x1, Pallas kernels, main_products(): pl.pallas_call(lambda *refs: main_kernel(scale, *refs), name='main_part',...  2.82 us
    ppermute x1, starting transfers between devices, body(): lax.ppermute(head_of(y_tiles), 'tm', [(i, i - 1) for i in range(1, tm)])  1.29 us
    pallas_call x1, Pallas kernels, head_of(): pl.pallas_call(head_kernel, name='head_part', in_specs=[pl.BlockSpec(memo...  0.94 us
    pallas_call x1, Pallas kernels, edge_products(): pl.pallas_call(edge_kernel, name='edge_part', in_specs=vmem(4), out_specs...  0.81 us
    reduce_sum x1, other arithmetic, body(): return jnp.sum(received, axis=0)  0.63 us
  transfers between devices with their start and end apart: 1, of which 1 were waited for; matrix products, arithmetic and copies ran while one was open for 0% of the time, Pallas kernels for 11%

profile of v4, /device:TPU:0, one launch (start us, length us, event | category | flops | bytes accessed | tf_op | source)
XLA Modules:
  0.0 26.2 jit_solution(13162063005439674064)
XLA Ops:
  0.0 0.0 copy-start
  0.0 0.0 copy-start.1
  0.0 0.9 %head_part.1 = f32[4,32,128]{2,1,0:T(8,128)S(1)} custom-call(f32[4,256,128]{2,1,0:T(8,128)} %bitcast.13), custom_call_target="tpu_custom_call" | custom-call | flops 10000000000 | tf_op jit(solution)/shard_map/head_part/pallas_call | solution.py:301
  0.9 1.3 %collective-permute-start = (f32[4,32,128]{2,1,0:T(8,128)S(1)}, f32[4,32,128]{2,1,0:T(8,128)S(1)}, u32[]{:S(2)}, u32[]{:S(2)}) collective-permute-start(f32[4,32,128]{2,1,0:T(8,128)S(1)} %head_part.1), channel_id=1, source_target_pairs={{4,0},{8,4},{12,8},{16,12},{20,16},{24,20},{28,24},{5,1},{9,5},{13... | collective-permute-start | bytes 196616 | tf_op jit(solution)/shard_map/ppermute | solution.py:352
  2.3 0.0 copy-done
  2.3 0.0 copy-done.1
  2.3 2.8 %main_part.1 = (f32[4,8,512]{2,1,0:T(8,128)S(1)}, bf16[4,128,256]{2,1,0:T(8,128)(2,1)S(1)}, bf16[4,128,256]{2,1,0:T(8,128)(2,1)S(1)}) custom-call(f32[4,256,128]{2,1,0:T(8,128)S(1)} %bitcast.15, f32[4,256,128]{2,1,0:T(8,128)S(1)} %bitcast.14), custom_call_target="tpu_custom_call" | custom-call | flops 402653184 | bytes 1048576 | tf_op jit(solution)/shard_map/main_part/pallas_call | solution.py:319
  5.1 3.0 %collective-permute-done.h_ref = f32[4,32,128]{2,1,0:T(8,128)S(1)} collective-permute-done((f32[4,32,128]{2,1,0:T(8,128)S(1)}, f32[4,32,128]{2,1,0:T(8,128)S(1)}, u32[]{:S(2)}, u32[]{:S(2)}) %collective-permute-start) | collective-permute-done | bytes 65568 | tf_op jit(solution)/shard_map/ppermute | solution.py:352
  8.1 0.8 %edge_part.1 = f32[4,8,512]{2,1,0:T(8,128)S(1)} custom-call(f32[4,32,128]{2,1,0:T(8,128)S(1)} %collective-permute-done.h_ref, bf16[4,128,256]{2,1,0:T(8,128)(2,1)S(1)} %get-tuple-element.8.th_ref, bf16[4,128,256]{2,1,0:T(8,128)(2,1)S(1)} %get-tuple-element.9.tl_ref, f32[4,8,512]{2,1,0:T(8,128)S(1)} %get-tuple-element.10.m_ref), custom_call_target="tpu_custom_call" | custom-call | tf_op jit(solution)/shard_map/edge_part/pallas_call | solution.py:337
  9.0 16.6 %all_to_all.5 = f32[32,16,128]{2,1,0:T(8,128)S(1)} all-to-all(f32[32,16,128]{2,1,0:T(8,128)S(1)} %bitcast.16), channel_id=1, replica_groups=mesh['tm'=8,'pair'=4] {'tm','pair'}, dimensions={0} | all-to-all | bytes 524288 | tf_op jit(solution)/shard_map/all_to_all | solution.py:364
  25.6 0.6 %reduce_sum.9 = f32[16,128]{1,0:T(8,128)} reduce(f32[32,16,128]{2,1,0:T(8,128)S(1)} %all_to_all.5, f32[]{:T(128)} %constant.5.clone.1), dimensions={0}, to_apply=%region_0.0 | reduce | flops 63488 | bytes 270340 | tf_op jit(solution)/shard_map/reduce_sum | solution.py:365
  (3 shorter events, 0.1 us)
Async XLA Ops:
  0.0 2.3 %copy-start = (f32[32,4096]{1,0:T(8,128)S(1)}, f32[32,4096]{1,0:T(8,128)}, u32[]{:S(2)}) copy-start(f32[32,4096]{1,0:T(8,128)} %param.3) | copy-start | bytes 1572868
  0.0 2.3 %copy-start.1 = (f32[32,4096]{1,0:T(8,128)S(1)}, f32[32,4096]{1,0:T(8,128)}, u32[]{:S(2)}) copy-start(f32[32,4096]{1,0:T(8,128)} %param.2) | copy-start | bytes 1572868
  0.9 7.1 %collective-permute-start = (f32[4,32,128]{2,1,0:T(8,128)S(1)}, f32[4,32,128]{2,1,0:T(8,128)S(1)}, u32[]{:S(2)}, u32[]{:S(2)}) collective-permute-start(f32[4,32,128]{2,1,0:T(8,128)S(1)} %head_part.1), channel_id=1, source_target_pairs={{4,0},{8,4},{12,8},{16,12},{20,16},{24,20},{28,24},{5,1},{9,5},{13... | collective-permute-start | bytes 196616 | tf_op jit(solution)/shard_map/ppermute | solution.py:352

commit v5 on v4

--- a/solution.py
+++ b/solution.py
@@ -346,7 +346,8 @@
 
 
 def body(x, y):
-    tm, pair = lax.axis_size("tm"), lax.axis_size("pair")
+    tm, high, low = (lax.axis_size(axis) for axis in AXES)
+    pair = high * low
     pairs_here, length = x.shape
     x_tiles, y_tiles = tiles_of(x), tiles_of(y)
     halo = lax.ppermute(head_of(y_tiles), "tm", [(i, i - 1) for i in range(1, tm)])
@@ -356,17 +357,30 @@
     out_rows = pairs_here * pair // tm
     out_cols = L // pair
     blocks_here = pairs_here // out_rows
-    mine = partial.reshape(blocks_here, out_rows, pair, out_cols).transpose(0, 2, 1, 3)
-    send = jnp.zeros((tm, pair, out_rows, out_cols), jnp.float32)
-    place = lax.axis_index("pair") * blocks_here
+    mine = partial.reshape(blocks_here, out_rows, high, low, out_cols).transpose(3, 0, 2, 1, 4)
+    if low == 2:
+        me = lax.axis_index("low")
+        away = lax.ppermute(
+            lax.dynamic_index_in_dim(mine, 1 - me, 0, keepdims=False), "low", [(0, 1), (1, 0)]
+        )
+        home = lax.dynamic_index_in_dim(mine, me, 0, keepdims=False)
+        mine = jnp.where(me == 0, jnp.stack([home, away]), jnp.stack([away, home]))
+    mine = mine.reshape(low * blocks_here, high, out_rows, out_cols)
+    send = jnp.zeros((tm, high, out_rows, out_cols), jnp.float32)
+    place = lax.axis_index("high") * low * blocks_here
     send = lax.dynamic_update_slice(send, mine, (place, 0, 0, 0))
-    send = send.reshape(tm * pair, out_rows, out_cols)
-    received = lax.all_to_all(send, ("tm", "pair"), 0, 0, tiled=True)
+    send = send.reshape(tm * high, out_rows, out_cols)
+    received = lax.all_to_all(send, ("tm", "high"), 0, 0, tiled=True)
     return jnp.sum(received, axis=0)
 
 
+AXES = ("tm", "high", "low")
+
+
 def solution(mesh):
-    specs = (P("pair", "tm"), P("pair", "tm"))
-    return jax.shard_map(
-        body, mesh=mesh, in_specs=specs, out_specs=P("tm", "pair"), check_vma=False
-    )
+    tm, pair = mesh.devices.shape
+    low = 2 if pair % 2 == 0 else 1
+    fine = jax.sharding.Mesh(mesh.devices.reshape(tm, pair // low, low), AXES)
+    spec = P(("high", "low"), "tm")
+    out = P("tm", ("high", "low"))
+    return jax.shard_map(body, mesh=fine, in_specs=(spec, spec), out_specs=out, check_vma=False)

time: 26.4 us -> 26 us (0.985)
  blocking collectives: 16.6 us -> 14.8 us
  waiting for transfers between devices: 2.99 us -> 4.18 us
    all_to_all x1, blocking collectives: 16.6 us -> 14.8 us  [body(): received = lax.all_to_all(send, ('tm', 'high'), 0, 0, tiled=True)]
    ppermute x0 -> x1, waiting for transfers between devices: none -> 1.18 us  [body(): lax.ppermute(lax.dynamic_index_in_dim(mine, 1 - me, 0, keepdims=False), '...]
  transfers between devices with their start and end apart: 1 -> 2, of which waited for: 1 -> 2; matrix products, arithmetic and copies ran while one was open for 0% -> 0% of each run, Pallas kernels for 11% -> 11%
where the time goes in v5:
time: 26 us; the launch traced here: 25.9 us
  blocking collectives  14.8 us (57%)
  Pallas kernels  4.56 us (18%)
  waiting for transfers between devices  4.18 us (16%)
  starting transfers between devices  1.36 us (5%)
  other arithmetic  0.65 us (2%)
    all_to_all x1, blocking collectives, body(): received = lax.all_to_all(send, ('tm', 'high'), 0, 0, tiled=True)  14.8 us
    ppermute x1, waiting for transfers between devices, body(): lax.ppermute(head_of(y_tiles), 'tm', [(i, i - 1) for i in range(1, tm)])  3 us
    pallas_call x1, Pallas kernels, main_products(): pl.pallas_call(lambda *refs: main_kernel(scale, *refs), name='main_part',...  2.81 us
    ppermute x1, starting transfers between devices, body(): lax.ppermute(head_of(y_tiles), 'tm', [(i, i - 1) for i in range(1, tm)])  1.29 us
    ppermute x1, waiting for transfers between devices, body(): lax.ppermute(lax.dynamic_index_in_dim(mine, 1 - me, 0, keepdims=False), '...  1.18 us
    pallas_call x1, Pallas kernels, head_of(): pl.pallas_call(head_kernel, name='head_part', in_specs=[pl.BlockSpec(memo...  0.94 us
    pallas_call x1, Pallas kernels, edge_products(): pl.pallas_call(edge_kernel, name='edge_part', in_specs=vmem(4), out_specs...  0.81 us
    reduce_sum x1, other arithmetic, body(): return jnp.sum(received, axis=0)  0.62 us
  transfers between devices with their start and end apart: 2, of which 2 were waited for; matrix products, arithmetic and copies ran while one was open for 0% of the time, Pallas kernels for 11%

profile of v5, /device:TPU:0, one launch (start us, length us, event | category | flops | bytes accessed | tf_op | source)
XLA Modules:
  0.0 25.9 jit_solution(13614322898908870411)
XLA Ops:
  0.0 0.0 copy-start
  0.0 0.0 copy-start.1
  0.0 0.9 %head_part.1 = f32[4,32,128]{2,1,0:T(8,128)S(1)} custom-call(f32[4,256,128]{2,1,0:T(8,128)} %bitcast.19), custom_call_target="tpu_custom_call" | custom-call | flops 10000000000 | tf_op jit(solution)/shard_map/head_part/pallas_call | solution.py:301
  0.9 1.3 %collective-permute-start = (f32[4,32,128]{2,1,0:T(8,128)S(1)}, f32[4,32,128]{2,1,0:T(8,128)S(1)}, u32[]{:S(2)}, u32[]{:S(2)}) collective-permute-start(f32[4,32,128]{2,1,0:T(8,128)S(1)} %head_part.1), channel_id=1, source_target_pairs={{4,0},{8,4},{12,8},{16,12},{20,16},{24,20},{28,24},{5,1},{9,5},{13... | collective-permute-start | bytes 196616 | tf_op jit(solution)/shard_map/ppermute | solution.py:353
  2.3 0.0 copy-done
  2.3 0.0 copy-done.1
  2.3 2.8 %main_part.1 = (f32[4,8,512]{2,1,0:T(8,128)S(1)}, bf16[4,128,256]{2,1,0:T(8,128)(2,1)S(1)}, bf16[4,128,256]{2,1,0:T(8,128)(2,1)S(1)}) custom-call(f32[4,256,128]{2,1,0:T(8,128)S(1)} %bitcast.21, f32[4,256,128]{2,1,0:T(8,128)S(1)} %bitcast.20), custom_call_target="tpu_custom_call" | custom-call | flops 402653184 | bytes 1048576 | tf_op jit(solution)/shard_map/main_part/pallas_call | solution.py:319
  5.1 3.0 %collective-permute-done.h_ref = f32[4,32,128]{2,1,0:T(8,128)S(1)} collective-permute-done((f32[4,32,128]{2,1,0:T(8,128)S(1)}, f32[4,32,128]{2,1,0:T(8,128)S(1)}, u32[]{:S(2)}, u32[]{:S(2)}) %collective-permute-start) | collective-permute-done | bytes 65568 | tf_op jit(solution)/shard_map/ppermute | solution.py:353
  8.1 0.8 %edge_part.1 = f32[4,8,512]{2,1,0:T(8,128)S(1)} custom-call(f32[4,32,128]{2,1,0:T(8,128)S(1)} %collective-permute-done.h_ref, bf16[4,128,256]{2,1,0:T(8,128)(2,1)S(1)} %get-tuple-element.8.th_ref, bf16[4,128,256]{2,1,0:T(8,128)(2,1)S(1)} %get-tuple-element.9.tl_ref, f32[4,8,512]{2,1,0:T(8,128)S(1)} %get-tuple-element.10.m_ref), custom_call_target="tpu_custom_call" | custom-call | tf_op jit(solution)/shard_map/edge_part/pallas_call | solution.py:337
  9.0 0.1 constant_dynamic-slice_fusion.1
  9.0 0.1 collective-permute-start.1
  9.1 1.2 %collective-permute-done.1 = f32[2,2,16,128]{3,1,2,0:T(2,128)S(1)} collective-permute-done((f32[2,2,16,128]{3,1,2,0:T(2,128)S(1)}, f32[2,2,16,128]{3,1,2,0:T(2,128)S(1)}, u32[]{:S(2)}, u32[]{:S(2)}) %collective-permute-start.1) | collective-permute-done | bytes 32800 | tf_op jit(solution)/shard_map/ppermute | solution.py:363
  10.4 14.8 %all_to_all.5 = f32[16,16,128]{2,1,0:T(8,128)S(1)} all-to-all(f32[16,16,128]{2,1,0:T(8,128)S(1)} %bitcast.22), channel_id=1, replica_groups=mesh['tm'=8,'high'=2,'low'=2] {'tm','high'}, dimensions={0} | all-to-all | bytes 262144 | tf_op jit(solution)/shard_map/all_to_all | solution.py:373
  25.2 0.6 %reduce_sum.9 = f32[16,128]{1,0:T(8,128)} reduce(f32[16,16,128]{2,1,0:T(8,128)S(1)} %all_to_all.5, f32[]{:T(128)} %constant.9.clone.1), dimensions={0}, to_apply=%region_0.1 | reduce | flops 30720 | bytes 139268 | tf_op jit(solution)/shard_map/reduce_sum | solution.py:374
  (5 shorter events, 0.1 us)
Async XLA Ops:
  0.0 2.3 %copy-start = (f32[32,4096]{1,0:T(8,128)S(1)}, f32[32,4096]{1,0:T(8,128)}, u32[]{:S(2)}) copy-start(f32[32,4096]{1,0:T(8,128)} %param.3) | copy-start | bytes 1572868
  0.0 2.3 %copy-start.1 = (f32[32,4096]{1,0:T(8,128)S(1)}, f32[32,4096]{1,0:T(8,128)}, u32[]{:S(2)}) copy-start(f32[32,4096]{1,0:T(8,128)} %param.2) | copy-start | bytes 1572868
  0.9 7.1 %collective-permute-start = (f32[4,32,128]{2,1,0:T(8,128)S(1)}, f32[4,32,128]{2,1,0:T(8,128)S(1)}, u32[]{:S(2)}, u32[]{:S(2)}) collective-permute-start(f32[4,32,128]{2,1,0:T(8,128)S(1)} %head_part.1), channel_id=1, source_target_pairs={{4,0},{8,4},{12,8},{16,12},{20,16},{24,20},{28,24},{5,1},{9,5},{13... | collective-permute-start | bytes 196616 | tf_op jit(solution)/shard_map/ppermute | solution.py:353
  9.0 1.3 %collective-permute-start.1 = (f32[2,2,16,128]{3,1,2,0:T(2,128)S(1)}, f32[2,2,16,128]{3,1,2,0:T(2,128)S(1)}, u32[]{:S(2)}, u32[]{:S(2)}) collective-permute-start(f32[2,2,16,128]{3,1,2,0:T(2,128)S(1)} %bitcast.25), channel_id=1, source_target_pairs={{0,1},{1,0},{2,3},{3,2},{4,5},{5,4},{6,7},{7,6},{8,9},{9,8},{10,11... | collective-permute-start | bytes 98312 | tf_op jit(solution)/shard_map/ppermute | solution.py:363

commit v6 on v5

--- a/solution.py
+++ b/solution.py
@@ -44,26 +44,6 @@
     copy = pltpu.make_async_copy(y_hbm.at[:, : head_ref.shape[1], :], head_ref, sem)
     copy.start()
     copy.wait()
-
-
-def store_tiles(ref, p, value):
-    for o in range(ref.shape[0]):
-        ref[o, p * PITCH : p * PITCH + SUB, :] = value[:, o * LANES : (o + 1) * LANES]
-
-
-def strided_tiles(ref, s):
-    at = pl.ds(s, SUB, stride=PITCH)
-    return jnp.concatenate([ref[o, at, :] for o in range(ref.shape[0])], axis=1)
-
-
-def load_kernel(x_hbm, y_hbm, x_ref, y_ref, head_ref, sems):
-    fetch_y = pltpu.make_async_copy(y_hbm, y_ref, sems.at[0])
-    fetch_x = pltpu.make_async_copy(x_hbm, x_ref, sems.at[1])
-    fetch_y.start()
-    fetch_x.start()
-    fetch_y.wait()
-    head_ref[...] = y_ref[:, : head_ref.shape[1], :]
-    fetch_x.wait()
 
 
 def turned(eye, value):
@@ -208,7 +188,8 @@
             finish(g - 1)
 
 
-def edge_kernel(h_ref, th_ref, tl_ref, m_ref, o_ref, tot):
+def edge_kernel(h_ref, th_ref, tl_ref, m_ref, *rest):
+    outs, tot = rest[:-1], rest[-1]
     tiles = L // LANES
     steps = LANES // FINE
     lanes = lane_index((SUB, LANES))
@@ -276,7 +257,19 @@
         for s in range(SUB):
             moved = pltpu.roll(strided_tiles(own, s), SUB - s, 1)
             result = result + jnp.where(columns < SUB - s, 0.0, moved)
-        o_ref[g] = result
+        if len(outs) == 1:
+            outs[0][g] = result
+            return
+        kept, sent = outs
+        out_rows, out_cols = kept.shape[2:]
+        second = lax.axis_index("low") == 1
+        block, row = divmod(g * SUB, out_rows)
+        for at in range(kept.shape[1]):
+            start = 2 * at * out_cols
+            one = result[:, start : start + out_cols]
+            two = result[:, start + out_cols : start + 2 * out_cols]
+            kept[block, at, row : row + SUB, :] = jnp.where(second, two, one)
+            sent[block, at, row : row + SUB, :] = jnp.where(second, one, two)
 
     grams = multiply(0)
     for g in range(groups):
@@ -333,13 +326,13 @@
     )(x, y)
 
 
-def edge_products(halo, tail_high, tail_low, partial):
+def edge_products(halo, tail_high, tail_low, partial, shapes):
     return pl.pallas_call(
         edge_kernel,
         name="edge_part",
         in_specs=vmem(4),
-        out_specs=vmem(1)[0],
-        out_shape=jax.ShapeDtypeStruct(partial.shape, jnp.float32),
+        out_specs=vmem(len(shapes)),
+        out_shape=[jax.ShapeDtypeStruct(shape, jnp.float32) for shape in shapes],
         scratch_shapes=[pltpu.VMEM((2, L // LANES, SUB * PITCH, LANES), jnp.float32)],
         compiler_params=pltpu.CompilerParams(vmem_limit_bytes=8 << 20),
     )(halo, tail_high, tail_low, partial)
@@ -353,17 +346,21 @@
     halo = lax.ppermute(head_of(y_tiles), "tm", [(i, i - 1) for i in range(1, tm)])
     scale = 1.0 / math.sqrt(tm * length)
     partial, tail_high, tail_low = main_products(x_tiles, y_tiles, scale)
-    partial = edge_products(halo, tail_high, tail_low, partial)
     out_rows = pairs_here * pair // tm
     out_cols = L // pair
     blocks_here = pairs_here // out_rows
-    mine = partial.reshape(blocks_here, out_rows, high, low, out_cols).transpose(3, 0, 2, 1, 4)
+    me = lax.axis_index("low")
+    if low == 2 and out_rows % SUB == 0 and out_cols % LANES == 0:
+        shapes = [(blocks_here, high, out_rows, out_cols)] * 2
+        home, away = edge_products(halo, tail_high, tail_low, partial, shapes)
+    else:
+        (partial,) = edge_products(halo, tail_high, tail_low, partial, [partial.shape])
+        mine = partial.reshape(blocks_here, out_rows, high, low, out_cols).transpose(3, 0, 2, 1, 4)
+        home = lax.dynamic_index_in_dim(mine, me, 0, keepdims=False)
+        away = lax.dynamic_index_in_dim(mine, low - 1 - me, 0, keepdims=False)
+    mine = home[None]
     if low == 2:
-        me = lax.axis_index("low")
-        away = lax.ppermute(
-            lax.dynamic_index_in_dim(mine, 1 - me, 0, keepdims=False), "low", [(0, 1), (1, 0)]
-        )
-        home = lax.dynamic_index_in_dim(mine, me, 0, keepdims=False)
+        away = lax.ppermute(away, "low", [(0, 1), (1, 0)])
         mine = jnp.where(me == 0, jnp.stack([home, away]), jnp.stack([away, home]))
     mine = mine.reshape(low * blocks_here, high, out_rows, out_cols)
     send = jnp.zeros((tm, high, out_rows, out_cols), jnp.float32)

time: 26 us -> 25.9 us (level)
  no operation moved by 1% of the time
where the time goes in v6:
time: 25.9 us; the launch traced here: 25.7 us
  blocking collectives  14.8 us (57%)
  Pallas kernels  4.56 us (18%)
  waiting for transfers between devices  4.18 us (16%)
  starting transfers between devices  1.36 us (5%)
  other arithmetic  0.62 us (2%)
    all_to_all x1, blocking collectives, body(): received = lax.all_to_all(send, ('tm', 'high'), 0, 0, tiled=True)  14.8 us
    ppermute x1, waiting for transfers between devices, body(): lax.ppermute(head_of(y_tiles), 'tm', [(i, i - 1) for i in range(1, tm)])  3 us
    pallas_call x1, Pallas kernels, main_products(): pl.pallas_call(lambda *refs: main_kernel(scale, *refs), name='main_part',...  2.82 us
    ppermute x1, starting transfers between devices, body(): lax.ppermute(head_of(y_tiles), 'tm', [(i, i - 1) for i in range(1, tm)])  1.29 us
    ppermute x1, waiting for transfers between devices, body(): away = lax.ppermute(away, 'low', [(0, 1), (1, 0)])  1.19 us
    pallas_call x1, Pallas kernels, head_of(): pl.pallas_call(head_kernel, name='head_part', in_specs=[pl.BlockSpec(memo...  0.94 us
    pallas_call x1, Pallas kernels, edge_products(): pl.pallas_call(edge_kernel, name='edge_part', in_specs=vmem(4), out_specs...  0.81 us
    reduce_sum x1, other arithmetic, body(): return jnp.sum(received, axis=0)  0.62 us
  transfers between devices with their start and end apart: 2, of which 2 were waited for; matrix products, arithmetic and copies ran while one was open for 0% of the time, Pallas kernels for 11%

profile of v6, /device:TPU:0, one launch (start us, length us, event | category | flops | bytes accessed | tf_op | source)
XLA Modules:
  0.0 25.7 jit_solution(2029972963963780119)
XLA Ops:
  0.0 0.0 copy-start
  0.0 0.0 copy-start.1
  0.0 0.9 %head_part.1 = f32[4,32,128]{2,1,0:T(8,128)S(1)} custom-call(f32[4,256,128]{2,1,0:T(8,128)} %bitcast.15), custom_call_target="tpu_custom_call" | custom-call | flops 10000000000 | tf_op jit(solution)/shard_map/head_part/pallas_call | solution.py:294
  0.9 1.3 %collective-permute-start = (f32[4,32,128]{2,1,0:T(8,128)S(1)}, f32[4,32,128]{2,1,0:T(8,128)S(1)}, u32[]{:S(2)}, u32[]{:S(2)}) collective-permute-start(f32[4,32,128]{2,1,0:T(8,128)S(1)} %head_part.1), channel_id=1, source_target_pairs={{4,0},{8,4},{12,8},{16,12},{20,16},{24,20},{28,24},{5,1},{9,5},{13... | collective-permute-start | bytes 196616 | tf_op jit(solution)/shard_map/ppermute | solution.py:346
  2.2 0.0 copy-done
  2.3 0.0 copy-done.1
  2.3 2.8 %main_part.1 = (f32[4,8,512]{2,1,0:T(8,128)S(1)}, bf16[4,128,256]{2,1,0:T(8,128)(2,1)S(1)}, bf16[4,128,256]{2,1,0:T(8,128)(2,1)S(1)}) custom-call(f32[4,256,128]{2,1,0:T(8,128)S(1)} %bitcast.17, f32[4,256,128]{2,1,0:T(8,128)S(1)} %bitcast.16), custom_call_target="tpu_custom_call" | custom-call | flops 402653184 | bytes 1048576 | tf_op jit(solution)/shard_map/main_part/pallas_call | solution.py:312
  5.1 3.0 %collective-permute-done.h_ref = f32[4,32,128]{2,1,0:T(8,128)S(1)} collective-permute-done((f32[4,32,128]{2,1,0:T(8,128)S(1)}, f32[4,32,128]{2,1,0:T(8,128)S(1)}, u32[]{:S(2)}, u32[]{:S(2)}) %collective-permute-start) | collective-permute-done | bytes 65568 | tf_op jit(solution)/shard_map/ppermute | solution.py:346
  8.1 0.8 %edge_part.1 = (f32[2,2,16,128]{3,2,1,0:T(8,128)S(1)}, f32[2,2,16,128]{3,2,1,0:T(8,128)S(1)}) custom-call(f32[4,32,128]{2,1,0:T(8,128)S(1)} %collective-permute-done.h_ref, bf16[4,128,256]{2,1,0:T(8,128)(2,1)S(1)} %get-tuple-element.10.th_ref, bf16[4,128,256]{2,1,0:T(8,128)(2,1)S(1)} %get-tuple-element.11.tl_ref, f32[4,8,512]{2,1,0:T(8,128)S(1)} %get-tuple-element.12.m_ref), custom_call_target="tpu_custom_call" | custom-call | tf_op jit(solution)/shard_map/edge_part/pallas_call | solution.py:330
  8.9 0.1 collective-permute-start.1
  9.0 1.2 %collective-permute-done.1 = f32[2,2,16,128]{3,2,1,0:T(8,128)S(1)} collective-permute-done((f32[2,2,16,128]{3,2,1,0:T(8,128)S(1)}, f32[2,2,16,128]{3,2,1,0:T(8,128)S(1)}, u32[]{:S(2)}, u32[]{:S(2)}) %collective-permute-start.1) | collective-permute-done | bytes 32800 | tf_op jit(solution)/shard_map/ppermute | solution.py:363
  10.2 14.8 %all_to_all.5 = f32[16,16,128]{2,1,0:T(8,128)S(1)} all-to-all(f32[16,16,128]{2,1,0:T(8,128)S(1)} %bitcast.18), channel_id=1, replica_groups=mesh['tm'=8,'high'=2,'low'=2] {'tm','high'}, dimensions={0} | all-to-all | bytes 262144 | tf_op jit(solution)/shard_map/all_to_all | solution.py:370
  25.1 0.6 %reduce_sum.9 = f32[16,128]{1,0:T(8,128)} reduce(f32[16,16,128]{2,1,0:T(8,128)S(1)} %all_to_all.5, f32[]{:T(128)} %constant.5.clone.1), dimensions={0}, to_apply=%region_0.1 | reduce | flops 30720 | bytes 139268 | tf_op jit(solution)/shard_map/reduce_sum | solution.py:371
  (3 shorter events, 0.0 us)
Async XLA Ops:
  0.0 2.2 %copy-start = (f32[32,4096]{1,0:T(8,128)S(1)}, f32[32,4096]{1,0:T(8,128)}, u32[]{:S(2)}) copy-start(f32[32,4096]{1,0:T(8,128)} %param.3) | copy-start | bytes 1572868
  0.0 2.3 %copy-start.1 = (f32[32,4096]{1,0:T(8,128)S(1)}, f32[32,4096]{1,0:T(8,128)}, u32[]{:S(2)}) copy-start(f32[32,4096]{1,0:T(8,128)} %param.2) | copy-start | bytes 1572868
  0.9 7.1 %collective-permute-start = (f32[4,32,128]{2,1,0:T(8,128)S(1)}, f32[4,32,128]{2,1,0:T(8,128)S(1)}, u32[]{:S(2)}, u32[]{:S(2)}) collective-permute-start(f32[4,32,128]{2,1,0:T(8,128)S(1)} %head_part.1), channel_id=1, source_target_pairs={{4,0},{8,4},{12,8},{16,12},{20,16},{24,20},{28,24},{5,1},{9,5},{13... | collective-permute-start | bytes 196616 | tf_op jit(solution)/shard_map/ppermute | solution.py:346
  8.9 1.3 %collective-permute-start.1 = (f32[2,2,16,128]{3,2,1,0:T(8,128)S(1)}, f32[2,2,16,128]{3,2,1,0:T(8,128)S(1)}, u32[]{:S(2)}, u32[]{:S(2)}) collective-permute-start(f32[2,2,16,128]{3,2,1,0:T(8,128)S(1)} %get-tuple-element.14), channel_id=1, source_target_pairs={{0,1},{1,0},{2,3},{3,2},{4,5},{5,4},{6,7},{7,6},{8,9},{9,8},{10,11... | collective-permute-start | bytes 98312 | tf_op jit(solution)/shard_map/ppermute | solution.py:363

commit v7 on v6

--- a/solution.py
+++ b/solution.py
@@ -40,10 +40,8 @@
     return jnp.concatenate([ref[o, at, :] for o in range(ref.shape[0])], axis=1)
 
 
-def head_kernel(y_hbm, head_ref, sem):
-    copy = pltpu.make_async_copy(y_hbm.at[:, : head_ref.shape[1], :], head_ref, sem)
-    copy.start()
-    copy.wait()
+def gate_kernel(head_ref, out_ref):
+    pass
 
 
 def turned(eye, value):
@@ -290,17 +288,17 @@
 
 
 def head_of(y):
-    head = (y.shape[0], L // LANES * SUB, LANES)
+    head = tiles_of(y[:, :L])
     return pl.pallas_call(
-        head_kernel,
-        name="head_part",
-        in_specs=[pl.BlockSpec(memory_space=pltpu.HBM)],
+        gate_kernel,
+        name="gate_part",
+        in_specs=vmem(1),
         out_specs=vmem(1)[0],
-        out_shape=jax.ShapeDtypeStruct(head, jnp.float32),
-        scratch_shapes=[pltpu.SemaphoreType.DMA],
+        out_shape=jax.ShapeDtypeStruct(head.shape, jnp.float32),
+        input_output_aliases={0: 0},
         compiler_params=pltpu.CompilerParams(vmem_limit_bytes=4 << 20),
         cost_estimate=pl.CostEstimate(flops=FLOPS, bytes_accessed=0, transcendentals=0),
-    )(pltpu.with_memory_space_constraint(y, pltpu.HBM))
+    )(head)
 
 
 def main_products(x, y, scale):
@@ -343,7 +341,7 @@
     pair = high * low
     pairs_here, length = x.shape
     x_tiles, y_tiles = tiles_of(x), tiles_of(y)
-    halo = lax.ppermute(head_of(y_tiles), "tm", [(i, i - 1) for i in range(1, tm)])
+    halo = lax.ppermute(head_of(y), "tm", [(i, i - 1) for i in range(1, tm)])
     scale = 1.0 / math.sqrt(tm * length)
     partial, tail_high, tail_low = main_products(x_tiles, y_tiles, scale)
     out_rows = pairs_here * pair // tm

time: 25.9 us -> 25.9 us (level)
  Pallas kernels: 4.56 us -> 3.64 us
  local copies, waits for them, and re-layouts: 0.03 us -> 0.87 us
    pallas_call x1, Pallas kernels: 0.94 us -> 0.01 us  [head_of(): pl.pallas_call(gate_kernel, name='gate_part', in_specs=vmem(1), out_specs...]
    reshape x0 -> x1, local copies, waits for them, and re-layouts: none -> 0.84 us  [tiles_of(): return tiles.reshape(groups, blocks * SUB, LANES)]
where the time goes in v7:
time: 25.9 us; the launch traced here: 25.7 us
  blocking collectives  14.8 us (57%)
  waiting for transfers between devices  4.18 us (16%)
  Pallas kernels  3.64 us (14%)
  starting transfers between devices  1.49 us (6%)
  local copies, waits for them, and re-layouts  0.87 us (3%)
  other arithmetic  0.62 us (2%)
    all_to_all x1, blocking collectives, body(): received = lax.all_to_all(send, ('tm', 'high'), 0, 0, tiled=True)  14.8 us
    ppermute x1, waiting for transfers between devices, body(): halo = lax.ppermute(head_of(y), 'tm', [(i, i - 1) for i in range(1, tm)])  2.99 us
    pallas_call x1, Pallas kernels, main_products(): pl.pallas_call(lambda *refs: main_kernel(scale, *refs), name='main_part',...  2.82 us
    ppermute x1, starting transfers between devices, body(): halo = lax.ppermute(head_of(y), 'tm', [(i, i - 1) for i in range(1, tm)])  1.42 us
    ppermute x1, waiting for transfers between devices, body(): away = lax.ppermute(away, 'low', [(0, 1), (1, 0)])  1.19 us
    reshape x1, local copies, waits for them, and re-layouts, tiles_of(): return tiles.reshape(groups, blocks * SUB, LANES)  0.84 us
    pallas_call x1, Pallas kernels, edge_products(): pl.pallas_call(edge_kernel, name='edge_part', in_specs=vmem(4), out_specs...  0.81 us
    reduce_sum x1, other arithmetic, body(): return jnp.sum(received, axis=0)  0.62 us
  transfers between devices with their start and end apart: 2, of which 2 were waited for; matrix products, arithmetic and copies ran while one was open for 0% of the time, Pallas kernels for 11%

profile of v7, /device:TPU:0, one launch (start us, length us, event | category | flops | bytes accessed | tf_op | source)
XLA Modules:
  0.0 25.7 jit_solution(16851246156878323210)
XLA Ops:
  0.0 0.8 %slice_bitcast_fusion.head_ref = f32[4,32,128]{2,1,0:T(8,128)S(1)} fusion(f32[32,4096]{1,0:T(8,128)} %param.3), kind=kLoop, calls=%fused_computation.1 | loop fusion | bytes 131072 | tf_op jit(solution)/shard_map/reshape | solution.py:283
  0.8 0.0 copy-start
  0.8 0.0 copy-start.1
  0.9 1.4 %collective-permute-start = (f32[4,32,128]{2,1,0:T(8,128)S(1)}, f32[4,32,128]{2,1,0:T(8,128)S(1)}, u32[]{:S(2)}, u32[]{:S(2)}) collective-permute-start(f32[4,32,128]{2,1,0:T(8,128)S(1)} %gate_part.1), channel_id=1, source_target_pairs={{4,0},{8,4},{12,8},{16,12},{20,16},{24,20},{28,24},{5,1},{9,5},{13... | collective-permute-start | bytes 196616 | tf_op jit(solution)/shard_map/ppermute | solution.py:344
  2.3 0.0 copy-done
  2.3 0.0 copy-done.1
  2.3 2.8 %main_part.1 = (f32[4,8,512]{2,1,0:T(8,128)S(1)}, bf16[4,128,256]{2,1,0:T(8,128)(2,1)S(1)}, bf16[4,128,256]{2,1,0:T(8,128)(2,1)S(1)}) custom-call(f32[4,256,128]{2,1,0:T(8,128)S(1)} %bitcast.22, f32[4,256,128]{2,1,0:T(8,128)S(1)} %bitcast.21), custom_call_target="tpu_custom_call" | custom-call | flops 402653184 | bytes 1048576 | tf_op jit(solution)/shard_map/main_part/pallas_call | solution.py:310
  5.1 3.0 %collective-permute-done.h_ref = f32[4,32,128]{2,1,0:T(8,128)S(1)} collective-permute-done((f32[4,32,128]{2,1,0:T(8,128)S(1)}, f32[4,32,128]{2,1,0:T(8,128)S(1)}, u32[]{:S(2)}, u32[]{:S(2)}) %collective-permute-start) | collective-permute-done | bytes 65568 | tf_op jit(solution)/shard_map/ppermute | solution.py:344
  8.1 0.8 %edge_part.1 = (f32[2,2,16,128]{3,2,1,0:T(8,128)S(1)}, f32[2,2,16,128]{3,2,1,0:T(8,128)S(1)}) custom-call(f32[4,32,128]{2,1,0:T(8,128)S(1)} %collective-permute-done.h_ref, bf16[4,128,256]{2,1,0:T(8,128)(2,1)S(1)} %get-tuple-element.10.th_ref, bf16[4,128,256]{2,1,0:T(8,128)(2,1)S(1)} %get-tuple-element.11.tl_ref, f32[4,8,512]{2,1,0:T(8,128)S(1)} %get-tuple-element.12.m_ref), custom_call_target="tpu_custom_call" | custom-call | tf_op jit(solution)/shard_map/edge_part/pallas_call | solution.py:328
  9.0 0.1 collective-permute-start.1
  9.0 1.2 %collective-permute-done.1 = f32[2,2,16,128]{3,2,1,0:T(8,128)S(1)} collective-permute-done((f32[2,2,16,128]{3,2,1,0:T(8,128)S(1)}, f32[2,2,16,128]{3,2,1,0:T(8,128)S(1)}, u32[]{:S(2)}, u32[]{:S(2)}) %collective-permute-start.1) | collective-permute-done | bytes 32800 | tf_op jit(solution)/shard_map/ppermute | solution.py:361
  10.3 14.8 %all_to_all.5 = f32[16,16,128]{2,1,0:T(8,128)S(1)} all-to-all(f32[16,16,128]{2,1,0:T(8,128)S(1)} %bitcast.23), channel_id=1, replica_groups=mesh['tm'=8,'high'=2,'low'=2] {'tm','high'}, dimensions={0} | all-to-all | bytes 262144 | tf_op jit(solution)/shard_map/all_to_all | solution.py:368
  25.1 0.6 %reduce_sum.9 = f32[16,128]{1,0:T(8,128)} reduce(f32[16,16,128]{2,1,0:T(8,128)S(1)} %all_to_all.5, f32[]{:T(128)} %constant.5.clone.1), dimensions={0}, to_apply=%region_0.1 | reduce | flops 30720 | bytes 139268 | tf_op jit(solution)/shard_map/reduce_sum | solution.py:369
  (4 shorter events, 0.0 us)
Async XLA Ops:
  0.8 1.5 %copy-start = (f32[32,4096]{1,0:T(8,128)S(1)}, f32[32,4096]{1,0:T(8,128)}, u32[]{:S(2)}) copy-start(f32[32,4096]{1,0:T(8,128)} %param.3) | copy-start | bytes 1572868
  0.8 1.5 %copy-start.1 = (f32[32,4096]{1,0:T(8,128)S(1)}, f32[32,4096]{1,0:T(8,128)}, u32[]{:S(2)}) copy-start(f32[32,4096]{1,0:T(8,128)} %param.2) | copy-start | bytes 1572868
  0.9 7.3 %collective-permute-start = (f32[4,32,128]{2,1,0:T(8,128)S(1)}, f32[4,32,128]{2,1,0:T(8,128)S(1)}, u32[]{:S(2)}, u32[]{:S(2)}) collective-permute-start(f32[4,32,128]{2,1,0:T(8,128)S(1)} %gate_part.1), channel_id=1, source_target_pairs={{4,0},{8,4},{12,8},{16,12},{20,16},{24,20},{28,24},{5,1},{9,5},{13... | collective-permute-start | bytes 196616 | tf_op jit(solution)/shard_map/ppermute | solution.py:344
  9.0 1.3 %collective-permute-start.1 = (f32[2,2,16,128]{3,2,1,0:T(8,128)S(1)}, f32[2,2,16,128]{3,2,1,0:T(8,128)S(1)}, u32[]{:S(2)}, u32[]{:S(2)}) collective-permute-start(f32[2,2,16,128]{3,2,1,0:T(8,128)S(1)} %get-tuple-element.14), channel_id=1, source_target_pairs={{0,1},{1,0},{2,3},{3,2},{4,5},{5,4},{6,7},{7,6},{8,9},{9,8},{10,11... | collective-permute-start | bytes 98312 | tf_op jit(solution)/shard_map/ppermute | solution.py:361

commit v8 on v6

--- a/solution.py
+++ b/solution.py
@@ -363,11 +363,12 @@
         away = lax.ppermute(away, "low", [(0, 1), (1, 0)])
         mine = jnp.where(me == 0, jnp.stack([home, away]), jnp.stack([away, home]))
     mine = mine.reshape(low * blocks_here, high, out_rows, out_cols)
-    send = jnp.zeros((tm, high, out_rows, out_cols), jnp.float32)
+    mine = mine.transpose(1, 0, 2, 3)
+    send = jnp.zeros((high, tm, out_rows, out_cols), jnp.float32)
     place = lax.axis_index("high") * low * blocks_here
-    send = lax.dynamic_update_slice(send, mine, (place, 0, 0, 0))
+    send = lax.dynamic_update_slice(send, mine, (0, place, 0, 0))
     send = send.reshape(tm * high, out_rows, out_cols)
-    received = lax.all_to_all(send, ("tm", "high"), 0, 0, tiled=True)
+    received = lax.all_to_all(send, ("high", "tm"), 0, 0, tiled=True)
     return jnp.sum(received, axis=0)
 
 

time: 25.9 us -> 25.9 us (level)
  no operation moved by 1% of the time
where the time goes in v8:
time: 25.9 us; the launch traced here: 25.7 us
  blocking collectives  14.8 us (57%)
  Pallas kernels  4.56 us (18%)
  waiting for transfers between devices  4.18 us (16%)
  starting transfers between devices  1.36 us (5%)
  other arithmetic  0.62 us (2%)
    all_to_all x1, blocking collectives, body(): received = lax.all_to_all(send, ('high', 'tm'), 0, 0, tiled=True)  14.8 us
    ppermute x1, waiting for transfers between devices, body(): lax.ppermute(head_of(y_tiles), 'tm', [(i, i - 1) for i in range(1, tm)])  3 us
    pallas_call x1, Pallas kernels, main_products(): pl.pallas_call(lambda *refs: main_kernel(scale, *refs), name='main_part',...  2.82 us
    ppermute x1, starting transfers between devices, body(): lax.ppermute(head_of(y_tiles), 'tm', [(i, i - 1) for i in range(1, tm)])  1.29 us
    ppermute x1, waiting for transfers between devices, body(): away = lax.ppermute(away, 'low', [(0, 1), (1, 0)])  1.19 us
    pallas_call x1, Pallas kernels, head_of(): pl.pallas_call(head_kernel, name='head_part', in_specs=[pl.BlockSpec(memo...  0.94 us
    pallas_call x1, Pallas kernels, edge_products(): pl.pallas_call(edge_kernel, name='edge_part', in_specs=vmem(4), out_specs...  0.81 us
    reduce_sum x1, other arithmetic, body(): return jnp.sum(received, axis=0)  0.62 us
  transfers between devices with their start and end apart: 2, of which 2 were waited for; matrix products, arithmetic and copies ran while one was open for 0% of the time, Pallas kernels for 11%

profile of v8, /device:TPU:0, one launch (start us, length us, event | category | flops | bytes accessed | tf_op | source)
XLA Modules:
  0.0 25.7 jit_solution(3997121769543168182)
XLA Ops:
  0.0 0.0 copy-start
  0.0 0.0 copy-start.1
  0.0 0.9 %head_part.1 = f32[4,32,128]{2,1,0:T(8,128)S(1)} custom-call(f32[4,256,128]{2,1,0:T(8,128)} %bitcast.17), custom_call_target="tpu_custom_call" | custom-call | flops 10000000000 | tf_op jit(solution)/shard_map/head_part/pallas_call | solution.py:294
  0.9 1.3 %collective-permute-start = (f32[4,32,128]{2,1,0:T(8,128)S(1)}, f32[4,32,128]{2,1,0:T(8,128)S(1)}, u32[]{:S(2)}, u32[]{:S(2)}) collective-permute-start(f32[4,32,128]{2,1,0:T(8,128)S(1)} %head_part.1), channel_id=1, source_target_pairs={{4,0},{8,4},{12,8},{16,12},{20,16},{24,20},{28,24},{5,1},{9,5},{13... | collective-permute-start | bytes 196616 | tf_op jit(solution)/shard_map/ppermute | solution.py:346
  2.2 0.0 copy-done
  2.3 0.0 copy-done.1
  2.3 2.8 %main_part.1 = (f32[4,8,512]{2,1,0:T(8,128)S(1)}, bf16[4,128,256]{2,1,0:T(8,128)(2,1)S(1)}, bf16[4,128,256]{2,1,0:T(8,128)(2,1)S(1)}) custom-call(f32[4,256,128]{2,1,0:T(8,128)S(1)} %bitcast.19, f32[4,256,128]{2,1,0:T(8,128)S(1)} %bitcast.18), custom_call_target="tpu_custom_call" | custom-call | flops 402653184 | bytes 1048576 | tf_op jit(solution)/shard_map/main_part/pallas_call | solution.py:312
  5.1 3.0 %collective-permute-done.h_ref = f32[4,32,128]{2,1,0:T(8,128)S(1)} collective-permute-done((f32[4,32,128]{2,1,0:T(8,128)S(1)}, f32[4,32,128]{2,1,0:T(8,128)S(1)}, u32[]{:S(2)}, u32[]{:S(2)}) %collective-permute-start) | collective-permute-done | bytes 65568 | tf_op jit(solution)/shard_map/ppermute | solution.py:346
  8.1 0.8 %edge_part.1 = (f32[2,2,16,128]{3,2,1,0:T(8,128)S(1)}, f32[2,2,16,128]{3,2,1,0:T(8,128)S(1)}) custom-call(f32[4,32,128]{2,1,0:T(8,128)S(1)} %collective-permute-done.h_ref, bf16[4,128,256]{2,1,0:T(8,128)(2,1)S(1)} %get-tuple-element.10.th_ref, bf16[4,128,256]{2,1,0:T(8,128)(2,1)S(1)} %get-tuple-element.11.tl_ref, f32[4,8,512]{2,1,0:T(8,128)S(1)} %get-tuple-element.12.m_ref), custom_call_target="tpu_custom_call" | custom-call | tf_op jit(solution)/shard_map/edge_part/pallas_call | solution.py:330
  8.9 0.1 collective-permute-start.1
  9.0 1.2 %collective-permute-done.1 = f32[2,2,16,128]{3,2,1,0:T(8,128)S(1)} collective-permute-done((f32[2,2,16,128]{3,2,1,0:T(8,128)S(1)}, f32[2,2,16,128]{3,2,1,0:T(8,128)S(1)}, u32[]{:S(2)}, u32[]{:S(2)}) %collective-permute-start.1) | collective-permute-done | bytes 32800 | tf_op jit(solution)/shard_map/ppermute | solution.py:363
  10.2 14.8 %all_to_all.5 = f32[16,16,128]{2,1,0:T(8,128)S(1)} all-to-all(f32[16,16,128]{2,1,0:T(8,128)S(1)} %bitcast.20), channel_id=1, replica_groups=mesh['tm'=8,'high'=2,'low'=2] {'high','tm'}, dimensions={0} | all-to-all | bytes 262144 | tf_op jit(solution)/shard_map/all_to_all | solution.py:371
  25.1 0.6 %reduce_sum.9 = f32[16,128]{1,0:T(8,128)} reduce(f32[16,16,128]{2,1,0:T(8,128)S(1)} %all_to_all.5, f32[]{:T(128)} %constant.5.clone.1), dimensions={0}, to_apply=%region_0.1 | reduce | flops 30720 | bytes 139268 | tf_op jit(solution)/shard_map/reduce_sum | solution.py:372
  (3 shorter events, 0.0 us)
Async XLA Ops:
  0.0 2.2 %copy-start = (f32[32,4096]{1,0:T(8,128)S(1)}, f32[32,4096]{1,0:T(8,128)}, u32[]{:S(2)}) copy-start(f32[32,4096]{1,0:T(8,128)} %param.3) | copy-start | bytes 1572868
  0.0 2.3 %copy-start.1 = (f32[32,4096]{1,0:T(8,128)S(1)}, f32[32,4096]{1,0:T(8,128)}, u32[]{:S(2)}) copy-start(f32[32,4096]{1,0:T(8,128)} %param.2) | copy-start | bytes 1572868
  0.9 7.1 %collective-permute-start = (f32[4,32,128]{2,1,0:T(8,128)S(1)}, f32[4,32,128]{2,1,0:T(8,128)S(1)}, u32[]{:S(2)}, u32[]{:S(2)}) collective-permute-start(f32[4,32,128]{2,1,0:T(8,128)S(1)} %head_part.1), channel_id=1, source_target_pairs={{4,0},{8,4},{12,8},{16,12},{20,16},{24,20},{28,24},{5,1},{9,5},{13... | collective-permute-start | bytes 196616 | tf_op jit(solution)/shard_map/ppermute | solution.py:346
  8.9 1.3 %collective-permute-start.1 = (f32[2,2,16,128]{3,2,1,0:T(8,128)S(1)}, f32[2,2,16,128]{3,2,1,0:T(8,128)S(1)}, u32[]{:S(2)}, u32[]{:S(2)}) collective-permute-start(f32[2,2,16,128]{3,2,1,0:T(8,128)S(1)} %get-tuple-element.14), channel_id=1, source_target_pairs={{0,1},{1,0},{2,3},{3,2},{4,5},{5,4},{6,7},{7,6},{8,9},{9,8},{10,11... | collective-permute-start | bytes 98312 | tf_op jit(solution)/shard_map/ppermute | solution.py:363
